TPU v7x, 1024 devices: a whole 8x8x8 slice. The times are simulated.
1024 devices in a mesh: dp: 64 (over y, z), tensor: 16 (over x, core).
Axes of the slice: x: 8, y: 8, z: 8, core: 2. Of those that a mesh axis runs over, the one named last changes fastest.
Arguments:
- momentum: bfloat16 [64, 512, 8192], P(None, 'dp', 'tensor'), may hold values from -125 to 125
- master: float32 [64, 512, 8192], P(None, 'dp', 'tensor'), may hold values from -0.06 to 0.06
- owner_order: int32 [64], replicated, may hold values from 0 to 63, each once
Outputs:
- new_master: float32 [64, 512, 8192], P(None, 'dp', 'tensor')
- owned_update: bfloat16 [64, 512, 8192], P('dp', None, 'tensor')
Inputs may be any that keep to these rules, and one draw needn't show every extreme that they name: `owner_order`: each matrix appears in exactly one slot; slot j is owned by dp index j.
All inputs are finite; a program needn't handle non-finite values.
Results may differ from a plain program's by a relative error of at most 0.025.
Values may be sent and summed in bfloat16 or wider, within the bound.
No kernel may reach another device: no remote copies, remote signals or barrier semaphores. Data moves between devices by JAX's collectives and lax.ppermute only.
A program may use at most 32 MiB of HBM per device.

v0:
```python
import math

import jax
import jax.numpy as jnp
from jax import lax
from jax.sharding import PartitionSpec as P

D = 8192
KV_DIM = 512
ITERS = 3


learn_rate = 0.02
weight_decay = 0.1
norm_epsilon = 1e-07
quintic_first = 3.4445
quintic_second = -4.775
quintic_third = 2.0315


def summed_gram(partial_value):
    return lax.psum(partial_value.astype(jnp.bfloat16), "tensor").astype(jnp.float32)


def shards(momentum, master, owner_order):
    matrices = momentum.shape[0]
    slotted = jnp.take(momentum, owner_order, axis=0)
    owned = lax.all_to_all(slotted, "dp", split_axis=0, concat_axis=1, tiled=True)
    squares = lax.psum(jnp.sum(jnp.square(owned.astype(jnp.float32)), axis=(1, 2)), "tensor")
    inv_norm = 1.0 / (jnp.sqrt(squares) + norm_epsilon)
    current = (owned.astype(jnp.float32) * inv_norm[:, None, None]).astype(jnp.bfloat16)
    source = owned
    combined = current.astype(jnp.float32)
    for iteration in range(ITERS):
        partial_value = jnp.einsum(
            "mik,mjk->mij", source, source, preferred_element_type=jnp.float32
        )
        gram = summed_gram(partial_value)
        if iteration == 0:
            gram = gram * (inv_norm * inv_norm)[:, None, None]
        coupling = gram.astype(jnp.bfloat16)
        first = jnp.einsum(
            "mij,mjk->mik", coupling, current, preferred_element_type=jnp.float32
        ).astype(jnp.bfloat16)
        second = jnp.einsum("mij,mjk->mik", coupling, first, preferred_element_type=jnp.float32)
        combined = (
            quintic_first * current.astype(jnp.float32)
            + quintic_second * first.astype(jnp.float32)
            + quintic_third * second
        )
        if iteration + 1 < ITERS:
            current = combined.astype(jnp.bfloat16)
            source = current
    scale_out = 0.2 * math.sqrt(max(KV_DIM, D))
    owned_update = (scale_out * combined).astype(jnp.bfloat16)
    returned = lax.all_to_all(owned_update, "dp", split_axis=1, concat_axis=0, tiled=True)
    inverse = (
        jnp.zeros((matrices,), jnp.int32).at[owner_order].set(jnp.arange(matrices, dtype=jnp.int32))
    )
    by_matrix = jnp.take(returned, inverse, axis=0)
    new_master = master * (1.0 - learn_rate * weight_decay) - learn_rate * by_matrix.astype(
        jnp.float32
    )
    return (new_master, owned_update)


def solution(mesh):
    return jax.shard_map(
        shards,
        mesh=mesh,
        in_specs=(P(None, "dp", "tensor"), P(None, "dp", "tensor"), P()),
        out_specs=(P(None, "dp", "tensor"), P("dp", None, "tensor")),
        check_vma=False,
    )
```

profile of v0, /device:TPU:38, one launch (start us, length us, event | category | flops | bytes accessed | tf_op | source)
XLA Modules:
  0.0 473.1 jit_solution(13301557437910299772)
XLA Ops:
  7.2 0.0 copy-start
  7.2 0.0 copy-start.6
  7.2 0.0 all-reduce.4.cloned.1.call-start
  7.2 0.7 compare_select_fusion.1
  7.9 0.0 copy-done.6
  8.0 0.3 copy-done
  8.2 0.6 gather_fusion
  8.8 0.1 broadcast_select_fusion
  9.0 42.3 %all_to_all.24 = bf16[64,8,512]{2,1,0:T(8,128)(2,1)S(1)} all-to-all(bf16[64,8,512]{2,1,0:T(8,128)(2,1)S(1)} %broadcast_select_fusion), channel_id=1, replica_groups=mesh['dp'=64,'tensor'=16] {'dp'}, dimensions={0} | all-to-all | bytes 1048576 | tf_op jit(solution)/shard_map/all_to_all | solution.py:28
  51.3 1.3 fusion.8
  52.5 0.0 all-reduce.4.cloned.1.call-update
  52.6 0.0 all-reduce.6.cloned.1.call-start
  52.6 0.9 fusion.9
  53.5 22.9 %psum.28 = f32[1]{0:T(128)} all-reduce(f32[1]{0:T(128)} %bitcast.1), channel_id=1, replica_groups=mesh['dp'=64,'tensor'=16] {'tensor'}, use_global_device_ids=true, to_apply=%region_1.3 | all-reduce | flops 1 | bytes 8 | tf_op jit(solution)/shard_map/psum | solution.py:29
  77.1 89.9 %all-reduce.4.cloned.1.call-done = bf16[1,512,512]{2,1,0:T(8,128)(2,1)} async-done(((bf16[1,512,512]{2,1,0:T(8,128)(2,1)}), bf16[1,512,512]{2,1,0:T(8,128)(2,1)}) %all-reduce.4.cloned.1.call-update) | async-done | bytes 524304 | tf_op jit(solution)/shard_map/psum | solution.py:22
  167.0 0.0 copy-start.5
  167.0 1.6 convolution_convert_fusion.4
  168.6 0.0 copy-done.5
  168.6 0.5 fusion.4
  169.2 1.3 convolution_convert_fusion.3
  170.4 0.0 all-reduce.6.cloned.1.call-update
  170.5 0.0 all-reduce.8.cloned.1.call-start
  170.5 123.4 %all-reduce.6.cloned.1.call-done = bf16[512,512]{1,0:T(8,128)(2,1)} async-done(((bf16[512,512]{1,0:T(8,128)(2,1)}), bf16[512,512]{1,0:T(8,128)(2,1)}) %all-reduce.6.cloned.1.call-update) | async-done | bytes 524304 | tf_op jit(solution)/shard_map/psum | solution.py:22
  293.9 0.0 copy-start.3
  293.9 1.5 convolution_convert_fusion.2
  295.4 0.0 copy-done.3
  295.5 0.5 fusion.5
  296.0 1.3 convolution_convert_fusion.1
  297.2 0.0 all-reduce.8.cloned.1.call-update
  297.2 123.4 %all-reduce.8.cloned.1.call-done = bf16[512,512]{1,0:T(8,128)(2,1)} async-done(((bf16[512,512]{1,0:T(8,128)(2,1)}), bf16[512,512]{1,0:T(8,128)(2,1)}) %all-reduce.8.cloned.1.call-update) | async-done | bytes 524304 | tf_op jit(solution)/shard_map/psum | solution.py:22
  420.7 0.0 copy-start.4
  420.7 1.5 convolution_convert_fusion
  422.2 0.0 copy-done.4
  422.2 0.5 fusion.7
  422.8 0.0 copy-start.2
  422.8 0.8 copy.11
  423.6 0.0 copy-done.2
  423.6 0.5 broadcast.62
  424.1 3.8 reduce.1
  427.9 1.0 reshape.144
  428.9 14.1 %all-to-all-start.1 = ((bf16[64,2,2048]{2,1,0:T(2,128)(2,1)}), bf16[64,2,2048]{2,1,0:T(2,128)(2,1)S(1)}, u32[]{:S(2)}, u32[]{:S(2)}) async-start(bf16[64,2,2048]{2,1,0:T(2,128)(2,1)} %reshape.144), calls=%async_computation.1 | async-start | bytes 1048576 | tf_op jit(solution)/shard_map/all_to_all | solution.py:56
  443.1 0.8 scatter_custom_fusion
  443.9 19.7 %all-to-all-done.1 = bf16[64,2,2048]{2,1,0:T(2,128)(2,1)S(1)} async-done(((bf16[64,2,2048]{2,1,0:T(2,128)(2,1)}), bf16[64,2,2048]{2,1,0:T(2,128)(2,1)S(1)}, u32[]{:S(2)}, u32[]{:S(2)}) %all-to-all-start.1) | async-done | bytes 524320 | tf_op jit(solution)/shard_map/all_to_all | solution.py:56
  463.6 0.5 reshape.145
  464.1 0.0 copy-start.1
  464.1 0.1 copy.10
  464.2 0.6 gather_fusion.1
  464.8 0.5 copy-done.1
  465.3 1.2 multiply_subtract_fusion
  (6 shorter events, 0.0 us)
Async XLA Ops:
  7.2 1.1 copy-start
  7.2 0.8 copy-start.6
  7.2 159.8 %all-reduce.4.cloned.1.call-start = ((), (), s32[]{:S(2)}) async-start(), calls=%async_computation.2 | async-start | bytes 1048576 | tf_op jit(solution)/shard_map/psum | solution.py:22
  52.6 241.3 %all-reduce.6.cloned.1.call-start = ((), (), s32[]{:S(2)}) async-start(), calls=%async_computation.3 | async-start | bytes 1048576 | tf_op jit(solution)/shard_map/psum | solution.py:22
  167.0 1.6 copy-start.5
  170.5 250.2 %all-reduce.8.cloned.1.call-start = ((), (), s32[]{:S(2)}) async-start(), calls=%async_computation.4 | async-start | bytes 1048576 | tf_op jit(solution)/shard_map/psum | solution.py:22
  293.9 1.6 copy-start.3
  420.7 1.6 copy-start.4
  422.8 0.8 copy-start.2
  428.9 34.6 %all-to-all-start.1 = ((bf16[64,2,2048]{2,1,0:T(2,128)(2,1)}), bf16[64,2,2048]{2,1,0:T(2,128)(2,1)S(1)}, u32[]{:S(2)}, u32[]{:S(2)}) async-start(bf16[64,2,2048]{2,1,0:T(2,128)(2,1)} %reshape.144), calls=%async_computation.1 | async-start | bytes 1048576 | tf_op jit(solution)/shard_map/all_to_all | solution.py:56
  464.1 1.2 copy-start.1
Sparse Core Ops, SparseCore 0:
  52.7 114.3 all-reduce.3
  170.6 123.2 all-reduce.5
  297.4 123.2 all-reduce.7
where the time goes:
time: 473 us
  waiting for transfers between devices  356 us (75%)
  blocking collectives  65.2 us (14%)
  between operations  14.7 us (3%)
  starting transfers between devices  14.3 us (3%)
  matrix products  10 us (2%)
  other arithmetic  6.78 us (1%)
  local copies, waits for them, and re-layouts  5.72 us (1%)
    psum x3, waiting for transfers between devices, summed_gram(): lax.psum(partial_value.astype(jnp.bfloat16), 'tensor').astype(jnp.float32)  337 us
    all_to_all x1, blocking collectives, shards(): lax.all_to_all(slotted, 'dp', split_axis=0, concat_axis=1, tiled=True)  42.3 us
    psum x1, blocking collectives, shards(): lax.psum(jnp.sum(jnp.square(owned.astype(jnp.float32)), axis=(1, 2)), 'te...  22.9 us
    all_to_all x1, waiting for transfers between devices, shards(): lax.all_to_all(owned_update, 'dp', split_axis=1, concat_axis=0, tiled=True)  19.7 us
    all_to_all x1, starting transfers between devices, shards(): lax.all_to_all(owned_update, 'dp', split_axis=1, concat_axis=0, tiled=True)  14.1 us
  transfers between devices with their start and end apart: 4, of which 4 were waited for; matrix products, arithmetic and copies ran while one was open for 0% of the time, Pallas kernels for 0%

commit v1 on v0

v1 whole, which is shorter than its diff:
```python
import functools
import math

import jax
import jax.numpy as jnp
from jax import lax
from jax.experimental import pallas as pl
from jax.experimental.pallas import tpu as pltpu
from jax.sharding import Mesh
from jax.sharding import PartitionSpec as P

D = 8192
KV_DIM = 512
ITERS = 3

learn_rate = 0.02
weight_decay = 0.1
norm_epsilon = 1e-07
quintic_first = 3.4445
quintic_second = -4.775
quintic_third = 2.0315
scale_out = 0.2 * math.sqrt(max(KV_DIM, D))

EDGE = 128
BLOCKS = ((0, 0), (1, 1), (2, 2), (3, 3), (0, 1), (1, 2), (2, 3), (0, 3), (0, 2), (1, 3))
HALF = len(BLOCKS) // 2
HALF_ROWS = HALF * EDGE


def matmul(left, right):
    return lax.dot_general(left, right, (((1,), (0,)), ((), ())), preferred_element_type=jnp.float32)


def two_parts(value):
    high = value.astype(jnp.bfloat16)
    return high, (value - high.astype(jnp.float32)).astype(jnp.bfloat16)


def gram_kernel(core_ref, owned_ref, kept_ref, sent_ref):
    owned = owned_ref[...]
    gram = lax.dot_general(owned, owned, (((1,), (1,)), ((), ())), preferred_element_type=jnp.float32)
    gram = gram.astype(jnp.bfloat16)
    core = core_ref[0]
    for half in range(2):
        for place in range(HALF):
            row, column = BLOCKS[half * HALF + place]
            block = gram[row * EDGE : (row + 1) * EDGE, column * EDGE : (column + 1) * EDGE]
            rows = slice(place * EDGE, (place + 1) * EDGE)

            @pl.when(core == half)
            def _(block=block, rows=rows):
                kept_ref[rows, :] = block

            @pl.when(core != half)
            def _(block=block, rows=rows):
                sent_ref[rows, :] = block


def sum_kernel(parts_ref, spread_ref):
    count = parts_ref.shape[0]
    total = parts_ref[0].astype(jnp.float32)
    for part in range(1, count):
        total = total + parts_ref[part].astype(jnp.float32)
    total = total.astype(jnp.bfloat16)
    for part in range(count):
        spread_ref[part] = total


def update_kernel(core_ref, mine_ref, other_ref, owned_ref, update_ref, gram_ref, wide_ref):
    core = core_ref[0]
    for half in range(2):
        for place in range(HALF):
            row, column = BLOCKS[half * HALF + place]
            rows = slice(place * EDGE, (place + 1) * EDGE)
            mine, other = mine_ref[rows, :].astype(jnp.float32), other_ref[rows, :].astype(jnp.float32)
            block = jnp.where(core == half, mine, other)
            down, across = pl.ds(row * EDGE, EDGE), pl.ds(column * EDGE, EDGE)
            wide_ref[down, across] = block
            if row != column:
                wide_ref[across, down] = block.T
    gram = wide_ref[...]
    gram_ref[...] = gram.astype(jnp.bfloat16)
    edge = gram.shape[0]
    diagonal = lax.broadcasted_iota(jnp.int32, (edge, edge), 0) == lax.broadcasted_iota(jnp.int32, (edge, edge), 1)
    squares = jnp.sum(jnp.where(diagonal, gram, 0.0), axis=0, keepdims=True)
    squares = jnp.sum(squares, axis=1, keepdims=True)
    inv_norm = 1.0 / (jnp.sqrt(squares) + norm_epsilon)
    inv_square = inv_norm * inv_norm

    exact = gram_ref[...]
    coupling = gram * inv_square
    square = matmul(exact, exact) * (inv_square * inv_square)
    step = quintic_second * coupling + quintic_third * square
    owned = owned_ref[...]
    current = owned.astype(jnp.float32) * inv_norm
    high, low = two_parts(step)
    current = quintic_first * current + (matmul(high, owned) + matmul(low, owned)) * inv_norm
    product = (matmul(high, exact) + matmul(low, exact)) * inv_square
    for iteration in range(1, ITERS):
        product_high, product_low = two_parts(product)
        coupling = (
            quintic_first * quintic_first * coupling
            + 2.0 * quintic_first * product
            + matmul(high, product_high)
            + matmul(high, product_low)
            + matmul(low, product_high)
        )
        coupling_high, coupling_low = two_parts(coupling)
        square = (
            matmul(coupling_high, coupling_high)
            + matmul(coupling_high, coupling_low)
            + matmul(coupling_low, coupling_high)
        )
        step = quintic_second * coupling + quintic_third * square
        high, low = two_parts(step)
        if iteration + 1 < ITERS:
            product = (
                matmul(high, coupling_high) + matmul(high, coupling_low) + matmul(low, coupling_high)
            )
        rounded = current.astype(jnp.bfloat16)
        current = quintic_first * current + matmul(high, rounded) + matmul(low, rounded)
    update_ref[...] = (scale_out * current).astype(jnp.bfloat16)


def limit(mib):
    return pltpu.CompilerParams(vmem_limit_bytes=mib * 1024 * 1024)


def vmem():
    return pl.BlockSpec(memory_space=pltpu.VMEM)


def smem():
    return pl.BlockSpec(memory_space=pltpu.SMEM)


def shards(chips, momentum, master, owner_order):
    matrices, rows, columns = momentum.shape
    slots = matrices
    core = lax.axis_index("core").astype(jnp.int32).reshape(1)
    swap = ((0, 1), (1, 0))
    slotted = jnp.take(momentum, owner_order, axis=0, mode="clip")
    owned = lax.all_to_all(slotted, "dp", split_axis=0, concat_axis=0, tiled=True)
    owned = owned.reshape(slots * rows, columns)
    packed = jax.ShapeDtypeStruct((HALF_ROWS, EDGE), jnp.bfloat16)
    kept, sent = pl.pallas_call(
        gram_kernel,
        out_shape=(packed, packed),
        in_specs=[smem(), vmem()],
        out_specs=(vmem(), vmem()),
        compiler_params=limit(8),
        name="gram",
    )(core, owned)
    received = lax.ppermute(sent, "core", swap)
    pair = (kept.astype(jnp.float32) + received.astype(jnp.float32)).astype(jnp.bfloat16)
    pair = pair.reshape(chips, HALF_ROWS // chips, EDGE)
    parts = lax.all_to_all(pair, "x", split_axis=0, concat_axis=0, tiled=True)
    spread = pl.pallas_call(
        sum_kernel,
        out_shape=jax.ShapeDtypeStruct(parts.shape, jnp.bfloat16),
        in_specs=[vmem()],
        out_specs=vmem(),
        compiler_params=limit(4),
        name="sum",
    )(parts)
    mine = lax.all_to_all(spread, "x", split_axis=0, concat_axis=0, tiled=True)
    mine = mine.reshape(HALF_ROWS, EDGE)
    other = lax.ppermute(mine, "core", swap)
    edge = owned.shape[0]
    owned_update = pl.pallas_call(
        update_kernel,
        out_shape=jax.ShapeDtypeStruct(owned.shape, jnp.bfloat16),
        in_specs=[smem(), vmem(), vmem(), vmem()],
        out_specs=vmem(),
        scratch_shapes=[
            pltpu.VMEM((edge, edge), jnp.bfloat16),
            pltpu.VMEM((edge, edge), jnp.float32),
        ],
        compiler_params=limit(24),
        name="update",
    )(core, mine, other, owned)
    returned = lax.all_to_all(
        owned_update.reshape(slots, rows, columns), "dp", split_axis=0, concat_axis=0, tiled=True
    )
    inverse = (
        jnp.zeros((matrices,), jnp.int32)
        .at[owner_order]
        .set(jnp.arange(matrices, dtype=jnp.int32), mode="promise_in_bounds", unique_indices=True)
    )
    by_matrix = jnp.take(returned, inverse, axis=0, mode="clip")
    new_master = master * (1.0 - learn_rate * weight_decay) - learn_rate * by_matrix.astype(
        jnp.float32
    )
    return (new_master, owned_update[None])


def solution(mesh):
    owners, columns = mesh.devices.shape
    chips = columns // 2
    split = Mesh(mesh.devices.reshape(owners, chips, 2), ("dp", "x", "core"))
    tensor = ("x", "core")
    return jax.shard_map(
        functools.partial(shards, chips),
        mesh=split,
        in_specs=(P(None, "dp", tensor), P(None, "dp", tensor), P()),
        out_specs=(P(None, "dp", tensor), P("dp", None, tensor)),
        check_vma=False,
    )
```

time: 473 us -> 117 us (0.25)
  the two profiles are of different devices: /device:TPU:38 before, /device:TPU:32 now
where the time goes in v1:
time: 117 us; the launch traced here: 116 us
  waiting for transfers between devices  41 us (35%)
  starting transfers between devices  32.3 us (28%)
  blocking collectives  28.5 us (24%)
  Pallas kernels  8.71 us (7%)
  local copies, waits for them, and re-layouts  3.1 us (3%)
  other arithmetic  1.93 us (2%)
    all_to_all x1, starting transfers between devices, shards(): lax.all_to_all(slotted, 'dp', split_axis=0, concat_axis=0, tiled=True)  23.1 us
    all_to_all x1, waiting for transfers between devices, shards(): lax.all_to_all(slotted, 'dp', split_axis=0, concat_axis=0, tiled=True)  19.4 us
    all_to_all x1, waiting for transfers between devices, shards(): lax.all_to_all(owned_update.reshape(slots, rows, columns), 'dp', split_ax...  18.9 us
    all_to_all x1, blocking collectives, shards(): parts = lax.all_to_all(pair, 'x', split_axis=0, concat_axis=0, tiled=True)  16.6 us
    all_to_all x1, blocking collectives, shards(): mine = lax.all_to_all(spread, 'x', split_axis=0, concat_axis=0, tiled=True)  11.8 us
    pallas_call x1, Pallas kernels, shards(): pl.pallas_call(update_kernel, out_shape=jax.ShapeDtypeStruct(owned.shape,...  8.13 us
    all_to_all x1, starting transfers between devices, shards(): lax.all_to_all(owned_update.reshape(slots, rows, columns), 'dp', split_ax...  5.36 us
  transfers between devices with their start and end apart: 4, of which 4 were waited for; matrix products, arithmetic and copies ran while one was open for 1% of the time, Pallas kernels for 0%

profile of v1, /device:TPU:32, one launch (start us, length us, event | category | flops | bytes accessed | tf_op | source)
XLA Modules:
  0.0 116.2 jit_solution(68455558110929866)
XLA Ops:
  0.6 0.0 copy-start
  0.6 0.7 pad_clamp_fusion.1
  1.4 0.3 copy-done
  1.7 1.4 %gather_fusion = bf16[64,8,512]{2,1,0:T(8,128)(2,1)} fusion(bf16[64,8,512]{2,1,0:T(8,128)(2,1)S(1)} %copy-done, s32[1024]{0:T(1024)S(1)} %pad_clamp_fusion.1), kind=kCustom, calls=%fused_computation | custom fusion | bytes 1048832 | tf_op jit(solution)/shard_map/jit(_take)/gather | solution.py:142
  3.1 23.1 %all-to-all-start = ((bf16[64,8,512]{2,1,0:T(8,128)(2,1)}), bf16[64,8,512]{2,1,0:T(8,128)(2,1)S(1)}, u32[]{:S(2)}, u32[]{:S(2)}) async-start(bf16[64,8,512]{2,1,0:T(8,128)(2,1)} %gather_fusion), calls=%async_computation | async-start | bytes 1048576 | tf_op jit(solution)/shard_map/all_to_all | solution.py:143
  26.2 19.4 %all-to-all-done = bf16[64,8,512]{2,1,0:T(8,128)(2,1)S(1)} async-done(((bf16[64,8,512]{2,1,0:T(8,128)(2,1)}), bf16[64,8,512]{2,1,0:T(8,128)(2,1)S(1)}, u32[]{:S(2)}, u32[]{:S(2)}) %all-to-all-start) | async-done | bytes 524320 | tf_op jit(solution)/shard_map/all_to_all | solution.py:143
  45.6 0.5 gram.1
  46.1 1.9 %collective-permute-start = (bf16[640,128]{1,0:T(8,128)(2,1)S(1)}, bf16[640,128]{1,0:T(8,128)(2,1)S(1)}, u32[]{:S(2)}, u32[]{:S(2)}) collective-permute-start(bf16[640,128]{1,0:T(8,128)(2,1)S(1)} %get-tuple-element.5), channel_id=1, source_target_pairs={{0,1},{1,0},{2,3},{3,2},{4,5},{5,4},{6,7},{7,6},{8,9},{9,8},{10,11... | collective-permute-start | bytes 491528 | tf_op jit(solution)/shard_map/ppermute | solution.py:154
  48.0 1.4 %collective-permute-done = bf16[640,128]{1,0:T(8,128)(2,1)S(1)} collective-permute-done((bf16[640,128]{1,0:T(8,128)(2,1)S(1)}, bf16[640,128]{1,0:T(8,128)(2,1)S(1)}, u32[]{:S(2)}, u32[]{:S(2)}) %collective-permute-start) | collective-permute-done | bytes 163872 | tf_op jit(solution)/shard_map/ppermute | solution.py:154
  49.5 16.6 %all_to_all.20.parts_ref = bf16[8,80,128]{2,1,0:T(8,128)(2,1)S(1)} all-to-all(bf16[8,80,128]{2,1,0:T(8,128)(2,1)S(1)} %bitcast.13), channel_id=1, replica_groups=mesh['dp'=64,'x'=8,'core'=2] {'x'}, dimensions={0} | all-to-all | bytes 327680 | tf_op jit(solution)/shard_map/all_to_all | solution.py:157
  66.1 11.8 %all_to_all.21 = bf16[8,80,128]{2,1,0:T(8,128)(2,1)S(1)} all-to-all(bf16[8,80,128]{2,1,0:T(8,128)(2,1)S(1)} %sum.1), channel_id=1, replica_groups=mesh['dp'=64,'x'=8,'core'=2] {'x'}, dimensions={0} | all-to-all | bytes 327680 | tf_op jit(solution)/shard_map/all_to_all | solution.py:166
  77.9 1.9 %collective-permute-start.1 = (bf16[640,128]{1,0:T(8,128)(2,1)S(1)}, bf16[640,128]{1,0:T(8,128)(2,1)S(1)}, u32[]{:S(2)}, u32[]{:S(2)}) collective-permute-start(bf16[640,128]{1,0:T(8,128)(2,1)S(1)} %bitcast.9), channel_id=1, source_target_pairs={{0,1},{1,0},{2,3},{3,2},{4,5},{5,4},{6,7},{7,6},{8,9},{9,8},{10,11... | collective-permute-start | bytes 491528 | tf_op jit(solution)/shard_map/ppermute | solution.py:168
  79.9 1.4 %collective-permute-done.1.other_ref = bf16[640,128]{1,0:T(8,128)(2,1)S(1)} collective-permute-done((bf16[640,128]{1,0:T(8,128)(2,1)S(1)}, bf16[640,128]{1,0:T(8,128)(2,1)S(1)}, u32[]{:S(2)}, u32[]{:S(2)}) %collective-permute-start.1) | collective-permute-done | bytes 163872 | tf_op jit(solution)/shard_map/ppermute | solution.py:168
  81.2 0.0 copy-start.2
  81.2 8.1 %update.1 = bf16[512,512]{1,0:T(8,128)(2,1)} custom-call(s32[1]{0:T(128)} %bitcast.core_ref, bf16[640,128]{1,0:T(8,128)(2,1)S(1)} %bitcast.10, bf16[640,128]{1,0:T(8,128)(2,1)S(1)} %collective-permute-done.1.other_ref, bf16[512,512]{1,0:T(8,128)(2,1)S(1)} %bitcast.8), custom_call_target="tpu_custom_call" | custom-call | tf_op jit(solution)/shard_map/update/pallas_call | solution.py:170
  89.4 0.0 copy-start.1
  89.4 5.4 %all-to-all-start.3 = ((bf16[64,8,512]{2,1,0:T(8,128)(2,1)}), bf16[64,8,512]{2,1,0:T(8,128)(2,1)S(1)}, u32[]{:S(2)}, u32[]{:S(2)}) async-start(bf16[64,8,512]{2,1,0:T(8,128)(2,1)} %bitcast.11), calls=%async_computation.3 | async-start | bytes 1048576 | tf_op jit(solution)/shard_map/all_to_all | solution.py:182
  94.7 0.0 copy-done.2
  94.8 0.8 scatter_custom_fusion
  95.6 18.9 %all-to-all-done.3 = bf16[64,8,512]{2,1,0:T(8,128)(2,1)S(1)} async-done(((bf16[64,8,512]{2,1,0:T(8,128)(2,1)}), bf16[64,8,512]{2,1,0:T(8,128)(2,1)S(1)}, u32[]{:S(2)}, u32[]{:S(2)}) %all-to-all-start.3) | async-done | bytes 524320 | tf_op jit(solution)/shard_map/all_to_all | solution.py:182
  114.4 0.6 gather_fusion.1
  115.0 0.0 copy-done.1
  115.0 1.2 multiply_subtract_fusion
  (5 shorter events, 0.1 us)
Async XLA Ops:
  0.6 1.1 copy-start
  3.1 42.5 %all-to-all-start = ((bf16[64,8,512]{2,1,0:T(8,128)(2,1)}), bf16[64,8,512]{2,1,0:T(8,128)(2,1)S(1)}, u32[]{:S(2)}, u32[]{:S(2)}) async-start(bf16[64,8,512]{2,1,0:T(8,128)(2,1)} %gather_fusion), calls=%async_computation | async-start | bytes 1048576 | tf_op jit(solution)/shard_map/all_to_all | solution.py:143
  46.1 3.3 %collective-permute-start = (bf16[640,128]{1,0:T(8,128)(2,1)S(1)}, bf16[640,128]{1,0:T(8,128)(2,1)S(1)}, u32[]{:S(2)}, u32[]{:S(2)}) collective-permute-start(bf16[640,128]{1,0:T(8,128)(2,1)S(1)} %get-tuple-element.5), channel_id=1, source_target_pairs={{0,1},{1,0},{2,3},{3,2},{4,5},{5,4},{6,7},{7,6},{8,9},{9,8},{10,11... | collective-permute-start | bytes 491528 | tf_op jit(solution)/shard_map/ppermute | solution.py:154
  77.9 3.3 %collective-permute-start.1 = (bf16[640,128]{1,0:T(8,128)(2,1)S(1)}, bf16[640,128]{1,0:T(8,128)(2,1)S(1)}, u32[]{:S(2)}, u32[]{:S(2)}) collective-permute-start(bf16[640,128]{1,0:T(8,128)(2,1)S(1)} %bitcast.9), channel_id=1, source_target_pairs={{0,1},{1,0},{2,3},{3,2},{4,5},{5,4},{6,7},{7,6},{8,9},{9,8},{10,11... | collective-permute-start | bytes 491528 | tf_op jit(solution)/shard_map/ppermute | solution.py:168
  81.2 13.5 %copy-start.2 = (s32[64]{0:T(128)S(1)}, s32[64]{0:T(128)}, u32[]{:S(2)}) copy-start(s32[64]{0:T(128)} %param.5) | copy-start | bytes 772
  89.4 25.7 %copy-start.1 = (f32[64,8,512]{2,1,0:T(8,128)S(1)}, f32[64,8,512]{2,1,0:T(8,128)}, u32[]{:S(2)}) copy-start(f32[64,8,512]{2,1,0:T(8,128)} %param.4) | copy-start | bytes 3145732
  89.4 25.1 %all-to-all-start.3 = ((bf16[64,8,512]{2,1,0:T(8,128)(2,1)}), bf16[64,8,512]{2,1,0:T(8,128)(2,1)S(1)}, u32[]{:S(2)}, u32[]{:S(2)}) async-start(bf16[64,8,512]{2,1,0:T(8,128)(2,1)} %bitcast.11), calls=%async_computation.3 | async-start | bytes 1048576 | tf_op jit(solution)/shard_map/all_to_all | solution.py:182

commit v2 on v1

--- a/solution.py
+++ b/solution.py
@@ -66,60 +66,93 @@
         spread_ref[part] = total
 
 
-def update_kernel(core_ref, mine_ref, other_ref, owned_ref, update_ref, gram_ref, wide_ref):
+def matmuls(lefts, right):
+    total = matmul(lefts[0], right)
+    for left in lefts[1:]:
+        total = total + matmul(left, right)
+    return total
+
+
+def symmetric_product(lefts, right):
+    half = right.shape[0] // 2
+    upper = matmuls([left[:half] for left in lefts], right)
+    lower = matmuls([left[half:] for left in lefts], right[:, half:])
+    return upper, lower
+
+
+def whole(upper, lower):
+    half = lower.shape[0]
+    corner = upper[:, half:]
+    left = jnp.concatenate([upper[:, :half], corner.T], axis=0)
+    right = jnp.concatenate([corner, lower], axis=0)
+    return jnp.concatenate([left, right], axis=1)
+
+
+def update_kernel(core_ref, mine_ref, other_ref, owned_ref, update_ref, packed_ref, gram_ref):
     core = core_ref[0]
-    for half in range(2):
-        for place in range(HALF):
-            row, column = BLOCKS[half * HALF + place]
-            rows = slice(place * EDGE, (place + 1) * EDGE)
-            mine, other = mine_ref[rows, :].astype(jnp.float32), other_ref[rows, :].astype(jnp.float32)
-            block = jnp.where(core == half, mine, other)
-            down, across = pl.ds(row * EDGE, EDGE), pl.ds(column * EDGE, EDGE)
-            wide_ref[down, across] = block
-            if row != column:
-                wide_ref[across, down] = block.T
-    gram = wide_ref[...]
-    gram_ref[...] = gram.astype(jnp.bfloat16)
-    edge = gram.shape[0]
-    diagonal = lax.broadcasted_iota(jnp.int32, (edge, edge), 0) == lax.broadcasted_iota(jnp.int32, (edge, edge), 1)
-    squares = jnp.sum(jnp.where(diagonal, gram, 0.0), axis=0, keepdims=True)
-    squares = jnp.sum(squares, axis=1, keepdims=True)
+    packed_ref[pl.ds(pl.multiple_of(core * HALF_ROWS, HALF_ROWS), HALF_ROWS), :] = mine_ref[...]
+    packed_ref[pl.ds(pl.multiple_of((1 - core) * HALF_ROWS, HALF_ROWS), HALF_ROWS), :] = other_ref[...]
+    squares = jnp.zeros((EDGE, EDGE), jnp.float32)
+    diagonal = lax.broadcasted_iota(jnp.int32, (EDGE, EDGE), 0) == lax.broadcasted_iota(jnp.int32, (EDGE, EDGE), 1)
+    for place, (row, column) in enumerate(BLOCKS):
+        block = packed_ref[place * EDGE : (place + 1) * EDGE, :]
+        down, across = pl.ds(row * EDGE, EDGE), pl.ds(column * EDGE, EDGE)
+        gram_ref[down, across] = block
+        if row != column:
+            gram_ref[across, down] = block.T
+        else:
+            squares = squares + jnp.where(diagonal, block.astype(jnp.float32), 0.0)
+    squares = jnp.sum(jnp.sum(squares, axis=0, keepdims=True), axis=1, keepdims=True)
     inv_norm = 1.0 / (jnp.sqrt(squares) + norm_epsilon)
     inv_square = inv_norm * inv_norm
 
-    exact = gram_ref[...]
-    coupling = gram * inv_square
-    square = matmul(exact, exact) * (inv_square * inv_square)
-    step = quintic_second * coupling + quintic_third * square
+    gram = gram_ref[...]
+    half = gram.shape[0] // 2
+    coupling = (gram[:half].astype(jnp.float32) * inv_square, gram[half:, half:].astype(jnp.float32) * inv_square)
+    square = symmetric_product([gram], gram)
+    third = quintic_third * (inv_square * inv_square)
+    step = [quintic_second * c + third * s for c, s in zip(coupling, square)]
+    step = two_parts(whole(*step))
     owned = owned_ref[...]
-    current = owned.astype(jnp.float32) * inv_norm
-    high, low = two_parts(step)
-    current = quintic_first * current + (matmul(high, owned) + matmul(low, owned)) * inv_norm
-    product = (matmul(high, exact) + matmul(low, exact)) * inv_square
+    product = [p * inv_square for p in symmetric_product(step, gram)]
+    current = quintic_first * inv_norm * owned.astype(jnp.float32) + matmuls(step, owned) * inv_norm
     for iteration in range(1, ITERS):
-        product_high, product_low = two_parts(product)
-        coupling = (
-            quintic_first * quintic_first * coupling
-            + 2.0 * quintic_first * product
-            + matmul(high, product_high)
-            + matmul(high, product_low)
-            + matmul(low, product_high)
-        )
-        coupling_high, coupling_low = two_parts(coupling)
-        square = (
-            matmul(coupling_high, coupling_high)
-            + matmul(coupling_high, coupling_low)
-            + matmul(coupling_low, coupling_high)
-        )
-        step = quintic_second * coupling + quintic_third * square
-        high, low = two_parts(step)
+        high, low = two_parts(whole(*product))
+        coupling = [
+            quintic_first * quintic_first * c + 2.0 * quintic_first * p + (d + e)
+            for c, p, d, e in zip(
+                coupling, product, symmetric_product(step, high), symmetric_product(step[:1], low)
+            )
+        ]
+        rounded = whole(*coupling).astype(jnp.bfloat16)
+        square = symmetric_product([rounded], rounded)
+        step = [quintic_second * c + quintic_third * s for c, s in zip(coupling, square)]
+        step = two_parts(whole(*step))
         if iteration + 1 < ITERS:
-            product = (
-                matmul(high, coupling_high) + matmul(high, coupling_low) + matmul(low, coupling_high)
-            )
-        rounded = current.astype(jnp.bfloat16)
-        current = quintic_first * current + matmul(high, rounded) + matmul(low, rounded)
+            product = symmetric_product(step, rounded)
+        current = quintic_first * current + matmuls(step, current.astype(jnp.bfloat16))
     update_ref[...] = (scale_out * current).astype(jnp.bfloat16)
+
+
+def gather_kernel(order_ref, source_ref, slots_ref):
+    def body(slot, carry):
+        slots_ref[slot] = source_ref[order_ref[slot]]
+        return carry
+
+    lax.fori_loop(0, slots_ref.shape[0], body, 0, unroll=8)
+
+
+def master_kernel(order_ref, returned_ref, master_ref, out_ref, ready_ref, sem):
+    def body(slot, carry):
+        matrix = order_ref[slot]
+        ready_ref[matrix] = master_ref[matrix] * (1.0 - learn_rate * weight_decay) - learn_rate * returned_ref[
+            slot
+        ].astype(jnp.float32)
+        pltpu.make_async_copy(ready_ref.at[matrix], out_ref.at[matrix], sem).start()
+        return carry
+
+    lax.fori_loop(0, returned_ref.shape[0], body, 0, unroll=4)
+    pltpu.make_async_copy(ready_ref, out_ref, sem).wait()
 
 
 def limit(mib):
@@ -139,7 +172,14 @@
     slots = matrices
     core = lax.axis_index("core").astype(jnp.int32).reshape(1)
     swap = ((0, 1), (1, 0))
-    slotted = jnp.take(momentum, owner_order, axis=0, mode="clip")
+    slotted = pl.pallas_call(
+        gather_kernel,
+        out_shape=jax.ShapeDtypeStruct(momentum.shape, momentum.dtype),
+        in_specs=[smem(), vmem()],
+        out_specs=vmem(),
+        compiler_params=limit(4),
+        name="gather",
+    )(owner_order, momentum)
     owned = lax.all_to_all(slotted, "dp", split_axis=0, concat_axis=0, tiled=True)
     owned = owned.reshape(slots * rows, columns)
     packed = jax.ShapeDtypeStruct((HALF_ROWS, EDGE), jnp.bfloat16)
@@ -173,8 +213,8 @@
         in_specs=[smem(), vmem(), vmem(), vmem()],
         out_specs=vmem(),
         scratch_shapes=[
+            pltpu.VMEM((2 * HALF_ROWS, EDGE), jnp.bfloat16),
             pltpu.VMEM((edge, edge), jnp.bfloat16),
-            pltpu.VMEM((edge, edge), jnp.float32),
         ],
         compiler_params=limit(24),
         name="update",
@@ -182,15 +222,15 @@
     returned = lax.all_to_all(
         owned_update.reshape(slots, rows, columns), "dp", split_axis=0, concat_axis=0, tiled=True
     )
-    inverse = (
-        jnp.zeros((matrices,), jnp.int32)
-        .at[owner_order]
-        .set(jnp.arange(matrices, dtype=jnp.int32), mode="promise_in_bounds", unique_indices=True)
-    )
-    by_matrix = jnp.take(returned, inverse, axis=0, mode="clip")
-    new_master = master * (1.0 - learn_rate * weight_decay) - learn_rate * by_matrix.astype(
-        jnp.float32
-    )
+    new_master = pl.pallas_call(
+        master_kernel,
+        out_shape=jax.ShapeDtypeStruct(master.shape, jnp.float32),
+        in_specs=[smem(), vmem(), vmem()],
+        out_specs=pl.BlockSpec(memory_space=pl.ANY),
+        scratch_shapes=[pltpu.VMEM(master.shape, jnp.float32), pltpu.SemaphoreType.DMA],
+        compiler_params=limit(8),
+        name="master",
+    )(owner_order, returned, master)
     return (new_master, owned_update[None])
 
 

time: 117 us -> 115 us (0.983)
  blocking collectives: 28.5 us -> 53.5 us
  waiting for transfers between devices: 41 us -> 22.1 us
  starting transfers between devices: 32.3 us -> 27 us
  other arithmetic: 1.93 us -> 0.05 us
  local copies, waits for them, and re-layouts: 3.1 us -> 1.7 us
    all_to_all x0 -> x1, blocking collectives: none -> 25.1 us  [shards(): lax.all_to_all(owned_update.reshape(slots, rows, columns), 'dp', split_ax...]
    all_to_all x1 -> x0, waiting for transfers between devices: 18.9 us -> none  [shards(): lax.all_to_all(owned_update.reshape(slots, rows, columns), 'dp', split_ax...]
    all_to_all x1 -> x0, starting transfers between devices: 5.36 us -> none  [shards(): lax.all_to_all(owned_update.reshape(slots, rows, columns), 'dp', split_ax...]
    pallas_call x0 -> x2, Pallas kernels: none -> 2.94 us  [the longest x1 1.5 us: shards(): pl.pallas_call(master_kernel, out_shape=jax.ShapeDtypeStruct(master.shape...]
    pallas_call x1, Pallas kernels: 8.13 us -> 6.15 us  [shards(): pl.pallas_call(update_kernel, out_shape=jax.ShapeDtypeStruct(owned.shape,...]
    gather x2 -> x0, local copies, waits for them, and re-layouts: 1.98 us -> none  [the longest x1 1.39 us: shards(): slotted = jnp.take(momentum, owner_order, axis=0, mode='clip')]
    unnamed x6 -> x8, local copies, waits for them, and re-layouts: 0.34 us -> 1.7 us
  transfers between devices with their start and end apart: 4 -> 3, of which waited for: 4 -> 3; matrix products, arithmetic and copies ran while one was open for 1% -> 0% of each run, Pallas kernels for 0% -> 0%
where the time goes in v2:
time: 115 us
  blocking collectives  53.5 us (47%)
  starting transfers between devices  27 us (23%)
  waiting for transfers between devices  22.1 us (19%)
  Pallas kernels  9.66 us (8%)
  local copies, waits for them, and re-layouts  1.7 us (1%)
    all_to_all x1, blocking collectives, shards(): lax.all_to_all(owned_update.reshape(slots, rows, columns), 'dp', split_ax...  25.1 us
    all_to_all x1, starting transfers between devices, shards(): lax.all_to_all(slotted, 'dp', split_axis=0, concat_axis=0, tiled=True)  23.1 us
    all_to_all x1, waiting for transfers between devices, shards(): lax.all_to_all(slotted, 'dp', split_axis=0, concat_axis=0, tiled=True)  19.4 us
    all_to_all x1, blocking collectives, shards(): parts = lax.all_to_all(pair, 'x', split_axis=0, concat_axis=0, tiled=True)  16.6 us
    all_to_all x1, blocking collectives, shards(): mine = lax.all_to_all(spread, 'x', split_axis=0, concat_axis=0, tiled=True)  11.8 us
    pallas_call x1, Pallas kernels, shards(): pl.pallas_call(update_kernel, out_shape=jax.ShapeDtypeStruct(owned.shape,...  6.15 us
  transfers between devices with their start and end apart: 3, of which 3 were waited for; matrix products, arithmetic and copies ran while one was open for 0% of the time, Pallas kernels for 0%

profile of v2, /device:TPU:32, one launch (start us, length us, event | category | flops | bytes accessed | tf_op | source)
XLA Modules:
  0.0 114.8 jit_solution(5786965999059641686)
XLA Ops:
  0.6 0.0 copy-start.1
  0.6 1.0 copy-done.1
  1.7 0.0 copy-start.2
  1.7 0.7 copy-done.2
  2.3 1.4 %gather.1 = bf16[64,8,512]{2,1,0:T(8,128)(2,1)} custom-call(s32[64]{0:T(128)S(1)} %copy-done.2, bf16[64,8,512]{2,1,0:T(8,128)(2,1)S(1)} %copy-done.1), custom_call_target="tpu_custom_call" | custom-call | tf_op jit(solution)/shard_map/gather/pallas_call | solution.py:175
  3.8 23.1 %all-to-all-start = ((bf16[64,8,512]{2,1,0:T(8,128)(2,1)}), bf16[64,8,512]{2,1,0:T(8,128)(2,1)S(1)}, u32[]{:S(2)}, u32[]{:S(2)}) async-start(bf16[64,8,512]{2,1,0:T(8,128)(2,1)} %gather.1), calls=%async_computation | async-start | bytes 1048576 | tf_op jit(solution)/shard_map/all_to_all | solution.py:183
  26.8 19.4 %all-to-all-done = bf16[64,8,512]{2,1,0:T(8,128)(2,1)S(1)} async-done(((bf16[64,8,512]{2,1,0:T(8,128)(2,1)}), bf16[64,8,512]{2,1,0:T(8,128)(2,1)S(1)}, u32[]{:S(2)}, u32[]{:S(2)}) %all-to-all-start) | async-done | bytes 524320 | tf_op jit(solution)/shard_map/all_to_all | solution.py:183
  46.2 0.5 gram.1
  46.8 1.9 %collective-permute-start = (bf16[640,128]{1,0:T(8,128)(2,1)S(1)}, bf16[640,128]{1,0:T(8,128)(2,1)S(1)}, u32[]{:S(2)}, u32[]{:S(2)}) collective-permute-start(bf16[640,128]{1,0:T(8,128)(2,1)S(1)} %get-tuple-element.5), channel_id=1, source_target_pairs={{0,1},{1,0},{2,3},{3,2},{4,5},{5,4},{6,7},{7,6},{8,9},{9,8},{10,11... | collective-permute-start | bytes 491528 | tf_op jit(solution)/shard_map/ppermute | solution.py:194
  48.7 1.4 %collective-permute-done = bf16[640,128]{1,0:T(8,128)(2,1)S(1)} collective-permute-done((bf16[640,128]{1,0:T(8,128)(2,1)S(1)}, bf16[640,128]{1,0:T(8,128)(2,1)S(1)}, u32[]{:S(2)}, u32[]{:S(2)}) %collective-permute-start) | collective-permute-done | bytes 163872 | tf_op jit(solution)/shard_map/ppermute | solution.py:194
  50.1 16.6 %all_to_all.20.parts_ref = bf16[8,80,128]{2,1,0:T(8,128)(2,1)S(1)} all-to-all(bf16[8,80,128]{2,1,0:T(8,128)(2,1)S(1)} %bitcast.12), channel_id=1, replica_groups=mesh['dp'=64,'x'=8,'core'=2] {'x'}, dimensions={0} | all-to-all | bytes 327680 | tf_op jit(solution)/shard_map/all_to_all | solution.py:197
  66.8 11.8 %all_to_all.21 = bf16[8,80,128]{2,1,0:T(8,128)(2,1)S(1)} all-to-all(bf16[8,80,128]{2,1,0:T(8,128)(2,1)S(1)} %sum.1), channel_id=1, replica_groups=mesh['dp'=64,'x'=8,'core'=2] {'x'}, dimensions={0} | all-to-all | bytes 327680 | tf_op jit(solution)/shard_map/all_to_all | solution.py:206
  78.6 0.0 copy-start
  78.6 2.0 %collective-permute-start.1 = (bf16[640,128]{1,0:T(8,128)(2,1)S(1)}, bf16[640,128]{1,0:T(8,128)(2,1)S(1)}, u32[]{:S(2)}, u32[]{:S(2)}) collective-permute-start(bf16[640,128]{1,0:T(8,128)(2,1)S(1)} %bitcast.8), channel_id=1, source_target_pairs={{0,1},{1,0},{2,3},{3,2},{4,5},{5,4},{6,7},{7,6},{8,9},{9,8},{10,11... | collective-permute-start | bytes 491528 | tf_op jit(solution)/shard_map/ppermute | solution.py:208
  80.7 1.4 %collective-permute-done.1.other_ref = bf16[640,128]{1,0:T(8,128)(2,1)S(1)} collective-permute-done((bf16[640,128]{1,0:T(8,128)(2,1)S(1)}, bf16[640,128]{1,0:T(8,128)(2,1)S(1)}, u32[]{:S(2)}, u32[]{:S(2)}) %collective-permute-start.1) | collective-permute-done | bytes 163872 | tf_op jit(solution)/shard_map/ppermute | solution.py:208
  82.0 6.2 %update.1 = bf16[512,512]{1,0:T(8,128)(2,1)} custom-call(s32[1]{0:T(128)} %bitcast.core_ref, bf16[640,128]{1,0:T(8,128)(2,1)S(1)} %bitcast.9, bf16[640,128]{1,0:T(8,128)(2,1)S(1)} %collective-permute-done.1.other_ref, bf16[512,512]{1,0:T(8,128)(2,1)S(1)} %bitcast.7), custom_call_target="tpu_custom_call" | custom-call | tf_op jit(solution)/shard_map/update/pallas_call | solution.py:210
  88.2 0.0 copy-start.3
  88.2 25.1 %all_to_all.22.returned_ref = bf16[64,8,512]{2,1,0:T(8,128)(2,1)S(1)} all-to-all(bf16[64,8,512]{2,1,0:T(8,128)(2,1)} %bitcast.10), channel_id=1, replica_groups=mesh['dp'=64,'x'=8,'core'=2] {'dp'}, dimensions={0} | all-to-all | bytes 1048576 | tf_op jit(solution)/shard_map/all_to_all | solution.py:222
  113.3 0.0 copy-done
  113.3 0.0 copy-done.3
  113.3 1.5 %master.1 = f32[64,8,512]{2,1,0:T(8,128)} custom-call(s32[64]{0:T(128)S(1)} %copy-done.3, bf16[64,8,512]{2,1,0:T(8,128)(2,1)S(1)} %all_to_all.22.returned_ref, f32[64,8,512]{2,1,0:T(8,128)S(1)} %copy-done), custom_call_target="tpu_custom_call" | custom-call | tf_op jit(solution)/shard_map/master/pallas_call | solution.py:225
  (2 shorter events, 0.1 us)
Async XLA Ops:
  0.6 1.0 copy-start.1
  1.7 0.7 copy-start.2
  3.8 42.5 %all-to-all-start = ((bf16[64,8,512]{2,1,0:T(8,128)(2,1)}), bf16[64,8,512]{2,1,0:T(8,128)(2,1)S(1)}, u32[]{:S(2)}, u32[]{:S(2)}) async-start(bf16[64,8,512]{2,1,0:T(8,128)(2,1)} %gather.1), calls=%async_computation | async-start | bytes 1048576 | tf_op jit(solution)/shard_map/all_to_all | solution.py:183
  46.8 3.3 %collective-permute-start = (bf16[640,128]{1,0:T(8,128)(2,1)S(1)}, bf16[640,128]{1,0:T(8,128)(2,1)S(1)}, u32[]{:S(2)}, u32[]{:S(2)}) collective-permute-start(bf16[640,128]{1,0:T(8,128)(2,1)S(1)} %get-tuple-element.5), channel_id=1, source_target_pairs={{0,1},{1,0},{2,3},{3,2},{4,5},{5,4},{6,7},{7,6},{8,9},{9,8},{10,11... | collective-permute-start | bytes 491528 | tf_op jit(solution)/shard_map/ppermute | solution.py:194
  78.6 34.6 %copy-start = (f32[64,8,512]{2,1,0:T(8,128)S(1)}, f32[64,8,512]{2,1,0:T(8,128)}, u32[]{:S(2)}) copy-start(f32[64,8,512]{2,1,0:T(8,128)} %master_ref.1) | copy-start | bytes 3145732
  78.6 3.4 %collective-permute-start.1 = (bf16[640,128]{1,0:T(8,128)(2,1)S(1)}, bf16[640,128]{1,0:T(8,128)(2,1)S(1)}, u32[]{:S(2)}, u32[]{:S(2)}) collective-permute-start(bf16[640,128]{1,0:T(8,128)(2,1)S(1)} %bitcast.8), channel_id=1, source_target_pairs={{0,1},{1,0},{2,3},{3,2},{4,5},{5,4},{6,7},{7,6},{8,9},{9,8},{10,11... | collective-permute-start | bytes 491528 | tf_op jit(solution)/shard_map/ppermute | solution.py:208
  88.2 25.1 %copy-start.3 = (s32[64]{0:T(128)S(1)}, s32[64]{0:T(128)}, u32[]{:S(2)}) copy-start(s32[64]{0:T(128)} %order_ref.3) | copy-start | bytes 772

commit v3 on v2

--- a/solution.py
+++ b/solution.py
@@ -22,9 +22,9 @@
 scale_out = 0.2 * math.sqrt(max(KV_DIM, D))
 
 EDGE = 128
-BLOCKS = ((0, 0), (1, 1), (2, 2), (3, 3), (0, 1), (1, 2), (2, 3), (0, 3), (0, 2), (1, 3))
-HALF = len(BLOCKS) // 2
-HALF_ROWS = HALF * EDGE
+MID = EDGE // 2
+PAIRS = ((0, 1), (1, 2), (2, 3), (0, 3), (0, 2), (1, 3))
+HALF_ROWS = (3 + len(PAIRS)) * EDGE // 2
 
 
 def matmul(left, right):
@@ -33,27 +33,47 @@
 
 def two_parts(value):
     high = value.astype(jnp.bfloat16)
-    return high, (value - high.astype(jnp.float32)).astype(jnp.bfloat16)
-
-
-def gram_kernel(core_ref, owned_ref, kept_ref, sent_ref):
+    return jnp.concatenate([high, (value - high.astype(jnp.float32)).astype(jnp.bfloat16)], axis=0)
+
+
+def both(parts, right):
+    rows = right.shape[0]
+    product = matmul(parts, right)
+    return product[:rows] + product[rows:]
+
+
+def halves(core):
+    return [pl.ds(pl.multiple_of(place * HALF_ROWS, HALF_ROWS), HALF_ROWS) for place in (core, 1 - core)]
+
+
+def tile_masks():
+    row = lax.broadcasted_iota(jnp.int32, (EDGE, EDGE), 0)
+    column = lax.broadcasted_iota(jnp.int32, (EDGE, EDGE), 1)
+    return row == column, (row >= MID) & (column < MID)
+
+
+def gram_kernel(core_ref, owned_ref, kept_ref, sent_ref, packed_ref):
     owned = owned_ref[...]
     gram = lax.dot_general(owned, owned, (((1,), (1,)), ((), ())), preferred_element_type=jnp.float32)
-    gram = gram.astype(jnp.bfloat16)
-    core = core_ref[0]
-    for half in range(2):
-        for place in range(HALF):
-            row, column = BLOCKS[half * HALF + place]
-            block = gram[row * EDGE : (row + 1) * EDGE, column * EDGE : (column + 1) * EDGE]
-            rows = slice(place * EDGE, (place + 1) * EDGE)
-
-            @pl.when(core == half)
-            def _(block=block, rows=rows):
-                kept_ref[rows, :] = block
-
-            @pl.when(core != half)
-            def _(block=block, rows=rows):
-                sent_ref[rows, :] = block
+
+    def block(row, column):
+        return gram[row * EDGE : (row + 1) * EDGE, column * EDGE : (column + 1) * EDGE]
+
+    _, lower_left = tile_masks()
+    fourth = block(3, 3)
+    shifted = pltpu.roll(fourth, MID, axis=1)
+    quarters = (
+        jnp.concatenate([fourth[MID:], fourth[:MID]], axis=0),
+        jnp.concatenate([shifted[MID:], shifted[:MID]], axis=0),
+        shifted,
+    )
+    tiles = [jnp.where(lower_left, quarter, block(place, place)) for place, quarter in enumerate(quarters)]
+    tiles += [block(row, column) for row, column in PAIRS]
+    for place, tile in enumerate(tiles):
+        packed_ref[place * EDGE : (place + 1) * EDGE, :] = tile.astype(jnp.bfloat16)
+    kept, sent = halves(core_ref[0])
+    kept_ref[...] = packed_ref[kept, :]
+    sent_ref[...] = packed_ref[sent, :]
 
 
 def sum_kernel(parts_ref, spread_ref):
@@ -66,71 +86,55 @@
         spread_ref[part] = total
 
 
-def matmuls(lefts, right):
-    total = matmul(lefts[0], right)
-    for left in lefts[1:]:
-        total = total + matmul(left, right)
-    return total
-
-
-def symmetric_product(lefts, right):
-    half = right.shape[0] // 2
-    upper = matmuls([left[:half] for left in lefts], right)
-    lower = matmuls([left[half:] for left in lefts], right[:, half:])
-    return upper, lower
-
-
-def whole(upper, lower):
-    half = lower.shape[0]
-    corner = upper[:, half:]
-    left = jnp.concatenate([upper[:, :half], corner.T], axis=0)
-    right = jnp.concatenate([corner, lower], axis=0)
-    return jnp.concatenate([left, right], axis=1)
-
-
 def update_kernel(core_ref, mine_ref, other_ref, owned_ref, update_ref, packed_ref, gram_ref):
-    core = core_ref[0]
-    packed_ref[pl.ds(pl.multiple_of(core * HALF_ROWS, HALF_ROWS), HALF_ROWS), :] = mine_ref[...]
-    packed_ref[pl.ds(pl.multiple_of((1 - core) * HALF_ROWS, HALF_ROWS), HALF_ROWS), :] = other_ref[...]
-    squares = jnp.zeros((EDGE, EDGE), jnp.float32)
-    diagonal = lax.broadcasted_iota(jnp.int32, (EDGE, EDGE), 0) == lax.broadcasted_iota(jnp.int32, (EDGE, EDGE), 1)
-    for place, (row, column) in enumerate(BLOCKS):
-        block = packed_ref[place * EDGE : (place + 1) * EDGE, :]
+    mine, other = halves(core_ref[0])
+    packed_ref[mine, :] = mine_ref[...]
+    packed_ref[other, :] = other_ref[...]
+
+    def tile(place):
+        return packed_ref[place * EDGE : (place + 1) * EDGE, :]
+
+    diagonal, lower_left = tile_masks()
+    blocks = [tile(place).astype(jnp.float32) for place in range(3)]
+    left = lax.broadcasted_iota(jnp.int32, (MID, EDGE), 1) < MID
+    first, second, third = (block[MID:] for block in blocks)
+    upper = jnp.where(left, first, pltpu.roll(second, MID, axis=1))
+    blocks.append(jnp.concatenate([upper, pltpu.roll(third, MID, axis=1)], axis=0))
+    squares = jnp.where(diagonal, blocks[0] + blocks[1] + blocks[2] + blocks[3], 0.0)
+    for place, block in enumerate(blocks):
+        at = pl.ds(place * EDGE, EDGE)
+        gram_ref[at, at] = jnp.where(lower_left, block.T, block).astype(jnp.bfloat16)
+    for place, (row, column) in enumerate(PAIRS):
+        block = tile(3 + place)
         down, across = pl.ds(row * EDGE, EDGE), pl.ds(column * EDGE, EDGE)
         gram_ref[down, across] = block
-        if row != column:
-            gram_ref[across, down] = block.T
-        else:
-            squares = squares + jnp.where(diagonal, block.astype(jnp.float32), 0.0)
+        gram_ref[across, down] = block.T
     squares = jnp.sum(jnp.sum(squares, axis=0, keepdims=True), axis=1, keepdims=True)
     inv_norm = 1.0 / (jnp.sqrt(squares) + norm_epsilon)
     inv_square = inv_norm * inv_norm
 
-    gram = gram_ref[...]
-    half = gram.shape[0] // 2
-    coupling = (gram[:half].astype(jnp.float32) * inv_square, gram[half:, half:].astype(jnp.float32) * inv_square)
-    square = symmetric_product([gram], gram)
-    third = quintic_third * (inv_square * inv_square)
-    step = [quintic_second * c + third * s for c, s in zip(coupling, square)]
-    step = two_parts(whole(*step))
+    factor = gram_ref[...]
+    edge = factor.shape[0]
+    coupling = factor.astype(jnp.float32) * inv_square
+    square = matmul(factor, factor) * (inv_square * inv_square)
+    step = two_parts(quintic_second * coupling + quintic_third * square)
+    product = both(step, factor) * inv_square
     owned = owned_ref[...]
-    product = [p * inv_square for p in symmetric_product(step, gram)]
-    current = quintic_first * inv_norm * owned.astype(jnp.float32) + matmuls(step, owned) * inv_norm
+    current = (quintic_first * owned.astype(jnp.float32) + both(step, owned)) * inv_norm
     for iteration in range(1, ITERS):
-        high, low = two_parts(whole(*product))
-        coupling = [
-            quintic_first * quintic_first * c + 2.0 * quintic_first * p + (d + e)
-            for c, p, d, e in zip(
-                coupling, product, symmetric_product(step, high), symmetric_product(step[:1], low)
-            )
-        ]
-        rounded = whole(*coupling).astype(jnp.bfloat16)
-        square = symmetric_product([rounded], rounded)
-        step = [quintic_second * c + quintic_third * s for c, s in zip(coupling, square)]
-        step = two_parts(whole(*step))
+        parts = two_parts(product)
+        coupling = (
+            quintic_first * quintic_first * coupling
+            + 2.0 * quintic_first * product
+            + both(step, parts[:edge])
+            + matmul(step[:edge], parts[edge:])
+        )
+        factor = coupling.astype(jnp.bfloat16)
+        square = matmul(factor, factor)
+        step = two_parts(quintic_second * coupling + quintic_third * square)
         if iteration + 1 < ITERS:
-            product = symmetric_product(step, rounded)
-        current = quintic_first * current + matmuls(step, current.astype(jnp.bfloat16))
+            product = both(step, factor)
+        current = quintic_first * current + both(step, current.astype(jnp.bfloat16))
     update_ref[...] = (scale_out * current).astype(jnp.bfloat16)
 
 
@@ -177,7 +181,6 @@
         out_shape=jax.ShapeDtypeStruct(momentum.shape, momentum.dtype),
         in_specs=[smem(), vmem()],
         out_specs=vmem(),
-        compiler_params=limit(4),
         name="gather",
     )(owner_order, momentum)
     owned = lax.all_to_all(slotted, "dp", split_axis=0, concat_axis=0, tiled=True)
@@ -188,6 +191,7 @@
         out_shape=(packed, packed),
         in_specs=[smem(), vmem()],
         out_specs=(vmem(), vmem()),
+        scratch_shapes=[pltpu.VMEM((2 * HALF_ROWS, EDGE), jnp.bfloat16)],
         compiler_params=limit(8),
         name="gram",
     )(core, owned)

time: 115 us -> 114 us (level)
  local copies, waits for them, and re-layouts: 1.7 us -> 0.01 us
    unnamed x8 -> x4, local copies, waits for them, and re-layouts: 1.7 us -> 0.01 us
where the time goes in v3:
time: 114 us; the launch traced here: 113 us
  blocking collectives  53 us (46%)
  starting transfers between devices  27 us (24%)
  waiting for transfers between devices  22.1 us (19%)
  Pallas kernels  10.6 us (9%)
    all_to_all x1, blocking collectives, shards(): lax.all_to_all(owned_update.reshape(slots, rows, columns), 'dp', split_ax...  25.1 us
    all_to_all x1, starting transfers between devices, shards(): lax.all_to_all(slotted, 'dp', split_axis=0, concat_axis=0, tiled=True)  23.1 us
    all_to_all x1, waiting for transfers between devices, shards(): lax.all_to_all(slotted, 'dp', split_axis=0, concat_axis=0, tiled=True)  19.4 us
    all_to_all x1, blocking collectives, shards(): parts = lax.all_to_all(pair, 'x', split_axis=0, concat_axis=0, tiled=True)  16.3 us
    all_to_all x1, blocking collectives, shards(): mine = lax.all_to_all(spread, 'x', split_axis=0, concat_axis=0, tiled=True)  11.6 us
    pallas_call x1, Pallas kernels, shards(): pl.pallas_call(update_kernel, out_shape=jax.ShapeDtypeStruct(owned.shape,...  6.54 us
  transfers between devices with their start and end apart: 3, of which 3 were waited for; matrix products, arithmetic and copies ran while one was open for 0% of the time, Pallas kernels for 0%

profile of v3, /device:TPU:32, one launch (start us, length us, event | category | flops | bytes accessed | tf_op | source)
XLA Modules:
  0.0 113.4 jit_solution(2872486257701759944)
XLA Ops:
  0.6 2.0 %gather.1 = bf16[64,8,512]{2,1,0:T(8,128)(2,1)} custom-call(s32[64]{0:T(128)} %order_ref.3, bf16[64,8,512]{2,1,0:T(8,128)(2,1)} %source_ref.1), custom_call_target="tpu_custom_call" | custom-call | tf_op jit(solution)/shard_map/gather/pallas_call | solution.py:179
  2.6 23.1 %all-to-all-start = ((bf16[64,8,512]{2,1,0:T(8,128)(2,1)}), bf16[64,8,512]{2,1,0:T(8,128)(2,1)S(1)}, u32[]{:S(2)}, u32[]{:S(2)}) async-start(bf16[64,8,512]{2,1,0:T(8,128)(2,1)} %gather.1), calls=%async_computation | async-start | bytes 1048576 | tf_op jit(solution)/shard_map/all_to_all | solution.py:186
  25.7 19.4 %all-to-all-done = bf16[64,8,512]{2,1,0:T(8,128)(2,1)S(1)} async-done(((bf16[64,8,512]{2,1,0:T(8,128)(2,1)}), bf16[64,8,512]{2,1,0:T(8,128)(2,1)S(1)}, u32[]{:S(2)}, u32[]{:S(2)}) %all-to-all-start) | async-done | bytes 524320 | tf_op jit(solution)/shard_map/all_to_all | solution.py:186
  45.1 0.6 gram.1
  45.6 1.9 %collective-permute-start = (bf16[576,128]{1,0:T(8,128)(2,1)S(1)}, bf16[576,128]{1,0:T(8,128)(2,1)S(1)}, u32[]{:S(2)}, u32[]{:S(2)}) collective-permute-start(bf16[576,128]{1,0:T(8,128)(2,1)S(1)} %get-tuple-element.5), channel_id=1, source_target_pairs={{0,1},{1,0},{2,3},{3,2},{4,5},{5,4},{6,7},{7,6},{8,9},{9,8},{10,11... | collective-permute-start | bytes 442376 | tf_op jit(solution)/shard_map/ppermute | solution.py:198
  47.6 1.3 %collective-permute-done = bf16[576,128]{1,0:T(8,128)(2,1)S(1)} collective-permute-done((bf16[576,128]{1,0:T(8,128)(2,1)S(1)}, bf16[576,128]{1,0:T(8,128)(2,1)S(1)}, u32[]{:S(2)}, u32[]{:S(2)}) %collective-permute-start) | collective-permute-done | bytes 147488 | tf_op jit(solution)/shard_map/ppermute | solution.py:198
  48.9 16.3 %all_to_all.20.parts_ref = bf16[8,72,128]{2,1,0:T(8,128)(2,1)S(1)} all-to-all(bf16[8,72,128]{2,1,0:T(8,128)(2,1)S(1)} %bitcast.12), channel_id=1, replica_groups=mesh['dp'=64,'x'=8,'core'=2] {'x'}, dimensions={0} | all-to-all | bytes 294912 | tf_op jit(solution)/shard_map/all_to_all | solution.py:201
  65.3 11.6 %all_to_all.21 = bf16[8,72,128]{2,1,0:T(8,128)(2,1)S(1)} all-to-all(bf16[8,72,128]{2,1,0:T(8,128)(2,1)S(1)} %sum.1), channel_id=1, replica_groups=mesh['dp'=64,'x'=8,'core'=2] {'x'}, dimensions={0} | all-to-all | bytes 294912 | tf_op jit(solution)/shard_map/all_to_all | solution.py:210
  76.9 0.0 copy-start
  76.9 2.0 %collective-permute-start.1 = (bf16[576,128]{1,0:T(8,128)(2,1)S(1)}, bf16[576,128]{1,0:T(8,128)(2,1)S(1)}, u32[]{:S(2)}, u32[]{:S(2)}) collective-permute-start(bf16[576,128]{1,0:T(8,128)(2,1)S(1)} %bitcast.8), channel_id=1, source_target_pairs={{0,1},{1,0},{2,3},{3,2},{4,5},{5,4},{6,7},{7,6},{8,9},{9,8},{10,11... | collective-permute-start | bytes 442376 | tf_op jit(solution)/shard_map/ppermute | solution.py:212
  78.9 1.3 %collective-permute-done.1.other_ref = bf16[576,128]{1,0:T(8,128)(2,1)S(1)} collective-permute-done((bf16[576,128]{1,0:T(8,128)(2,1)S(1)}, bf16[576,128]{1,0:T(8,128)(2,1)S(1)}, u32[]{:S(2)}, u32[]{:S(2)}) %collective-permute-start.1) | collective-permute-done | bytes 147488 | tf_op jit(solution)/shard_map/ppermute | solution.py:212
  80.3 6.5 %update.1 = bf16[512,512]{1,0:T(8,128)(2,1)} custom-call(s32[1]{0:T(128)} %bitcast.core_ref, bf16[576,128]{1,0:T(8,128)(2,1)S(1)} %bitcast.9, bf16[576,128]{1,0:T(8,128)(2,1)S(1)} %collective-permute-done.1.other_ref, bf16[512,512]{1,0:T(8,128)(2,1)S(1)} %bitcast.7), custom_call_target="tpu_custom_call" | custom-call | tf_op jit(solution)/shard_map/update/pallas_call | solution.py:214
  86.8 0.0 copy-start.1
  86.8 25.1 %all_to_all.22.returned_ref = bf16[64,8,512]{2,1,0:T(8,128)(2,1)S(1)} all-to-all(bf16[64,8,512]{2,1,0:T(8,128)(2,1)} %bitcast.10), channel_id=1, replica_groups=mesh['dp'=64,'x'=8,'core'=2] {'dp'}, dimensions={0} | all-to-all | bytes 1048576 | tf_op jit(solution)/shard_map/all_to_all | solution.py:226
  111.9 0.0 copy-done
  111.9 0.0 copy-done.1
  111.9 1.5 %master.1 = f32[64,8,512]{2,1,0:T(8,128)} custom-call(s32[64]{0:T(128)S(1)} %copy-done.1, bf16[64,8,512]{2,1,0:T(8,128)(2,1)S(1)} %all_to_all.22.returned_ref, f32[64,8,512]{2,1,0:T(8,128)S(1)} %copy-done), custom_call_target="tpu_custom_call" | custom-call | tf_op jit(solution)/shard_map/master/pallas_call | solution.py:229
  (2 shorter events, 0.1 us)
Async XLA Ops:
  2.6 42.5 %all-to-all-start = ((bf16[64,8,512]{2,1,0:T(8,128)(2,1)}), bf16[64,8,512]{2,1,0:T(8,128)(2,1)S(1)}, u32[]{:S(2)}, u32[]{:S(2)}) async-start(bf16[64,8,512]{2,1,0:T(8,128)(2,1)} %gather.1), calls=%async_computation | async-start | bytes 1048576 | tf_op jit(solution)/shard_map/all_to_all | solution.py:186
  45.6 3.3 %collective-permute-start = (bf16[576,128]{1,0:T(8,128)(2,1)S(1)}, bf16[576,128]{1,0:T(8,128)(2,1)S(1)}, u32[]{:S(2)}, u32[]{:S(2)}) collective-permute-start(bf16[576,128]{1,0:T(8,128)(2,1)S(1)} %get-tuple-element.5), channel_id=1, source_target_pairs={{0,1},{1,0},{2,3},{3,2},{4,5},{5,4},{6,7},{7,6},{8,9},{9,8},{10,11... | collective-permute-start | bytes 442376 | tf_op jit(solution)/shard_map/ppermute | solution.py:198
  76.9 35.0 %copy-start = (f32[64,8,512]{2,1,0:T(8,128)S(1)}, f32[64,8,512]{2,1,0:T(8,128)}, u32[]{:S(2)}) copy-start(f32[64,8,512]{2,1,0:T(8,128)} %master_ref.1) | copy-start | bytes 3145732
  76.9 3.4 %collective-permute-start.1 = (bf16[576,128]{1,0:T(8,128)(2,1)S(1)}, bf16[576,128]{1,0:T(8,128)(2,1)S(1)}, u32[]{:S(2)}, u32[]{:S(2)}) collective-permute-start(bf16[576,128]{1,0:T(8,128)(2,1)S(1)} %bitcast.8), channel_id=1, source_target_pairs={{0,1},{1,0},{2,3},{3,2},{4,5},{5,4},{6,7},{7,6},{8,9},{9,8},{10,11... | collective-permute-start | bytes 442376 | tf_op jit(solution)/shard_map/ppermute | solution.py:212
  86.8 25.1 %copy-start.1 = (s32[64]{0:T(128)S(1)}, s32[64]{0:T(128)}, u32[]{:S(2)}) copy-start(s32[64]{0:T(128)} %order_ref.3) | copy-start | bytes 772

commit v4 on v3

--- a/solution.py
+++ b/solution.py
@@ -33,13 +33,29 @@
 
 def two_parts(value):
     high = value.astype(jnp.bfloat16)
-    return jnp.concatenate([high, (value - high.astype(jnp.float32)).astype(jnp.bfloat16)], axis=0)
-
-
-def both(parts, right):
-    rows = right.shape[0]
-    product = matmul(parts, right)
-    return product[:rows] + product[rows:]
+    return high, (value - high.astype(jnp.float32)).astype(jnp.bfloat16)
+
+
+def matmuls(lefts, right):
+    total = matmul(lefts[0], right)
+    for left in lefts[1:]:
+        total = total + matmul(left, right)
+    return total
+
+
+def symmetric_product(lefts, right):
+    half = right.shape[0] // 2
+    upper = matmuls([left[:half] for left in lefts], right)
+    lower = matmuls([left[half:] for left in lefts], right[:, half:])
+    return upper, lower
+
+
+def whole(upper, lower):
+    half = lower.shape[0]
+    corner = upper[:, half:]
+    left = jnp.concatenate([upper[:, :half], corner.T], axis=0)
+    right = jnp.concatenate([corner, lower], axis=0)
+    return jnp.concatenate([left, right], axis=1)
 
 
 def halves(core):
@@ -114,28 +130,42 @@
     inv_square = inv_norm * inv_norm
 
     factor = gram_ref[...]
-    edge = factor.shape[0]
-    coupling = factor.astype(jnp.float32) * inv_square
-    square = matmul(factor, factor) * (inv_square * inv_square)
-    step = two_parts(quintic_second * coupling + quintic_third * square)
-    product = both(step, factor) * inv_square
-    owned = owned_ref[...]
-    current = (quintic_first * owned.astype(jnp.float32) + both(step, owned)) * inv_norm
+    half = factor.shape[0] // 2
+    coupling = [
+        factor[:half].astype(jnp.float32) * inv_square,
+        factor[half:, half:].astype(jnp.float32) * inv_square,
+    ]
+    square = symmetric_product([factor], factor)
+    third = quintic_third * (inv_square * inv_square)
+    step = [quintic_second * c + third * s for c, s in zip(coupling, square)]
+    step = two_parts(whole(*step))
+    operand = owned_ref[...]
+    product = [p * inv_square for p in symmetric_product(step, factor)]
+    current = (quintic_first * operand.astype(jnp.float32) + matmul(step[0], operand)) * inv_norm
+    rest_scale = inv_norm
     for iteration in range(1, ITERS):
-        parts = two_parts(product)
-        coupling = (
-            quintic_first * quintic_first * coupling
-            + 2.0 * quintic_first * product
-            + both(step, parts[:edge])
-            + matmul(step[:edge], parts[edge:])
-        )
-        factor = coupling.astype(jnp.bfloat16)
-        square = matmul(factor, factor)
-        step = two_parts(quintic_second * coupling + quintic_third * square)
+        high, low = two_parts(whole(*product))
+        coupling = [
+            quintic_first * quintic_first * c + 2.0 * quintic_first * p + (d + e)
+            for c, p, d, e in zip(
+                coupling, product, symmetric_product(step, high), symmetric_product(step[:1], low)
+            )
+        ]
+        current = current + matmul(step[1], operand) * rest_scale
+        operand = current.astype(jnp.bfloat16)
+        factor = whole(*coupling).astype(jnp.bfloat16)
         if iteration + 1 < ITERS:
-            product = both(step, factor)
-        current = quintic_first * current + both(step, current.astype(jnp.bfloat16))
-    update_ref[...] = (scale_out * current).astype(jnp.bfloat16)
+            square = symmetric_product([factor], factor)
+            step = [quintic_second * c + quintic_third * s for c, s in zip(coupling, square)]
+            step = two_parts(whole(*step))
+            product = symmetric_product(step, factor)
+            current = quintic_first * current + matmul(step[0], operand)
+            rest_scale = 1.0
+    first = matmul(factor, operand).astype(jnp.bfloat16)
+    for rows in (slice(0, half), slice(half, 2 * half)):
+        second = matmul(factor[rows], first)
+        update = quintic_first * current[rows] + quintic_second * first[rows].astype(jnp.float32) + quintic_third * second
+        update_ref[rows, :] = (scale_out * update).astype(jnp.bfloat16)
 
 
 def gather_kernel(order_ref, source_ref, slots_ref):

time: 114 us -> 113 us (level)
  no operation moved by 1% of the time
where the time goes in v4:
time: 113 us
  blocking collectives  53 us (47%)
  starting transfers between devices  27 us (24%)
  waiting for transfers between devices  22.1 us (20%)
  Pallas kernels  9.72 us (9%)
    all_to_all x1, blocking collectives, shards(): lax.all_to_all(owned_update.reshape(slots, rows, columns), 'dp', split_ax...  25.1 us
    all_to_all x1, starting transfers between devices, shards(): lax.all_to_all(slotted, 'dp', split_axis=0, concat_axis=0, tiled=True)  23.1 us
    all_to_all x1, waiting for transfers between devices, shards(): lax.all_to_all(slotted, 'dp', split_axis=0, concat_axis=0, tiled=True)  19.4 us
    all_to_all x1, blocking collectives, shards(): parts = lax.all_to_all(pair, 'x', split_axis=0, concat_axis=0, tiled=True)  16.3 us
    all_to_all x1, blocking collectives, shards(): mine = lax.all_to_all(spread, 'x', split_axis=0, concat_axis=0, tiled=True)  11.6 us
    pallas_call x1, Pallas kernels, shards(): pl.pallas_call(update_kernel, out_shape=jax.ShapeDtypeStruct(owned.shape,...  5.69 us
  transfers between devices with their start and end apart: 3, of which 3 were waited for; matrix products, arithmetic and copies ran while one was open for 0% of the time, Pallas kernels for 0%

profile of v4, /device:TPU:32, one launch (start us, length us, event | category | flops | bytes accessed | tf_op | source)
XLA Modules:
  0.0 112.5 jit_solution(3055448242837621101)
XLA Ops:
  0.6 2.0 %gather.1 = bf16[64,8,512]{2,1,0:T(8,128)(2,1)} custom-call(s32[64]{0:T(128)} %order_ref.3, bf16[64,8,512]{2,1,0:T(8,128)(2,1)} %source_ref.1), custom_call_target="tpu_custom_call" | custom-call | tf_op jit(solution)/shard_map/gather/pallas_call | solution.py:209
  2.6 23.1 %all-to-all-start = ((bf16[64,8,512]{2,1,0:T(8,128)(2,1)}), bf16[64,8,512]{2,1,0:T(8,128)(2,1)S(1)}, u32[]{:S(2)}, u32[]{:S(2)}) async-start(bf16[64,8,512]{2,1,0:T(8,128)(2,1)} %gather.1), calls=%async_computation | async-start | bytes 1048576 | tf_op jit(solution)/shard_map/all_to_all | solution.py:216
  25.7 19.4 %all-to-all-done = bf16[64,8,512]{2,1,0:T(8,128)(2,1)S(1)} async-done(((bf16[64,8,512]{2,1,0:T(8,128)(2,1)}), bf16[64,8,512]{2,1,0:T(8,128)(2,1)S(1)}, u32[]{:S(2)}, u32[]{:S(2)}) %all-to-all-start) | async-done | bytes 524320 | tf_op jit(solution)/shard_map/all_to_all | solution.py:216
  45.1 0.6 gram.1
  45.6 1.9 %collective-permute-start = (bf16[576,128]{1,0:T(8,128)(2,1)S(1)}, bf16[576,128]{1,0:T(8,128)(2,1)S(1)}, u32[]{:S(2)}, u32[]{:S(2)}) collective-permute-start(bf16[576,128]{1,0:T(8,128)(2,1)S(1)} %get-tuple-element.5), channel_id=1, source_target_pairs={{0,1},{1,0},{2,3},{3,2},{4,5},{5,4},{6,7},{7,6},{8,9},{9,8},{10,11... | collective-permute-start | bytes 442376 | tf_op jit(solution)/shard_map/ppermute | solution.py:228
  47.6 1.3 %collective-permute-done = bf16[576,128]{1,0:T(8,128)(2,1)S(1)} collective-permute-done((bf16[576,128]{1,0:T(8,128)(2,1)S(1)}, bf16[576,128]{1,0:T(8,128)(2,1)S(1)}, u32[]{:S(2)}, u32[]{:S(2)}) %collective-permute-start) | collective-permute-done | bytes 147488 | tf_op jit(solution)/shard_map/ppermute | solution.py:228
  48.9 16.3 %all_to_all.20.parts_ref = bf16[8,72,128]{2,1,0:T(8,128)(2,1)S(1)} all-to-all(bf16[8,72,128]{2,1,0:T(8,128)(2,1)S(1)} %bitcast.12), channel_id=1, replica_groups=mesh['dp'=64,'x'=8,'core'=2] {'x'}, dimensions={0} | all-to-all | bytes 294912 | tf_op jit(solution)/shard_map/all_to_all | solution.py:231
  65.3 11.6 %all_to_all.21 = bf16[8,72,128]{2,1,0:T(8,128)(2,1)S(1)} all-to-all(bf16[8,72,128]{2,1,0:T(8,128)(2,1)S(1)} %sum.1), channel_id=1, replica_groups=mesh['dp'=64,'x'=8,'core'=2] {'x'}, dimensions={0} | all-to-all | bytes 294912 | tf_op jit(solution)/shard_map/all_to_all | solution.py:240
  76.9 0.0 copy-start
  76.9 2.0 %collective-permute-start.1 = (bf16[576,128]{1,0:T(8,128)(2,1)S(1)}, bf16[576,128]{1,0:T(8,128)(2,1)S(1)}, u32[]{:S(2)}, u32[]{:S(2)}) collective-permute-start(bf16[576,128]{1,0:T(8,128)(2,1)S(1)} %bitcast.8), channel_id=1, source_target_pairs={{0,1},{1,0},{2,3},{3,2},{4,5},{5,4},{6,7},{7,6},{8,9},{9,8},{10,11... | collective-permute-start | bytes 442376 | tf_op jit(solution)/shard_map/ppermute | solution.py:242
  78.9 1.3 %collective-permute-done.1.other_ref = bf16[576,128]{1,0:T(8,128)(2,1)S(1)} collective-permute-done((bf16[576,128]{1,0:T(8,128)(2,1)S(1)}, bf16[576,128]{1,0:T(8,128)(2,1)S(1)}, u32[]{:S(2)}, u32[]{:S(2)}) %collective-permute-start.1) | collective-permute-done | bytes 147488 | tf_op jit(solution)/shard_map/ppermute | solution.py:242
  80.3 5.7 %update.1 = bf16[512,512]{1,0:T(8,128)(2,1)} custom-call(s32[1]{0:T(128)} %bitcast.core_ref, bf16[576,128]{1,0:T(8,128)(2,1)S(1)} %bitcast.9, bf16[576,128]{1,0:T(8,128)(2,1)S(1)} %collective-permute-done.1.other_ref, bf16[512,512]{1,0:T(8,128)(2,1)S(1)} %bitcast.7), custom_call_target="tpu_custom_call" | custom-call | tf_op jit(solution)/shard_map/update/pallas_call | solution.py:244
  86.0 0.0 copy-start.1
  86.0 25.1 %all_to_all.22.returned_ref = bf16[64,8,512]{2,1,0:T(8,128)(2,1)S(1)} all-to-all(bf16[64,8,512]{2,1,0:T(8,128)(2,1)} %bitcast.10), channel_id=1, replica_groups=mesh['dp'=64,'x'=8,'core'=2] {'dp'}, dimensions={0} | all-to-all | bytes 1048576 | tf_op jit(solution)/shard_map/all_to_all | solution.py:256
  111.0 0.0 copy-done
  111.0 0.0 copy-done.1
  111.0 1.5 %master.1 = f32[64,8,512]{2,1,0:T(8,128)} custom-call(s32[64]{0:T(128)S(1)} %copy-done.1, bf16[64,8,512]{2,1,0:T(8,128)(2,1)S(1)} %all_to_all.22.returned_ref, f32[64,8,512]{2,1,0:T(8,128)S(1)} %copy-done), custom_call_target="tpu_custom_call" | custom-call | tf_op jit(solution)/shard_map/master/pallas_call | solution.py:259
  (2 shorter events, 0.1 us)
Async XLA Ops:
  2.6 42.5 %all-to-all-start = ((bf16[64,8,512]{2,1,0:T(8,128)(2,1)}), bf16[64,8,512]{2,1,0:T(8,128)(2,1)S(1)}, u32[]{:S(2)}, u32[]{:S(2)}) async-start(bf16[64,8,512]{2,1,0:T(8,128)(2,1)} %gather.1), calls=%async_computation | async-start | bytes 1048576 | tf_op jit(solution)/shard_map/all_to_all | solution.py:216
  45.6 3.3 %collective-permute-start = (bf16[576,128]{1,0:T(8,128)(2,1)S(1)}, bf16[576,128]{1,0:T(8,128)(2,1)S(1)}, u32[]{:S(2)}, u32[]{:S(2)}) collective-permute-start(bf16[576,128]{1,0:T(8,128)(2,1)S(1)} %get-tuple-element.5), channel_id=1, source_target_pairs={{0,1},{1,0},{2,3},{3,2},{4,5},{5,4},{6,7},{7,6},{8,9},{9,8},{10,11... | collective-permute-start | bytes 442376 | tf_op jit(solution)/shard_map/ppermute | solution.py:228
  76.9 34.1 %copy-start = (f32[64,8,512]{2,1,0:T(8,128)S(1)}, f32[64,8,512]{2,1,0:T(8,128)}, u32[]{:S(2)}) copy-start(f32[64,8,512]{2,1,0:T(8,128)} %master_ref.1) | copy-start | bytes 3145732
  76.9 3.4 %collective-permute-start.1 = (bf16[576,128]{1,0:T(8,128)(2,1)S(1)}, bf16[576,128]{1,0:T(8,128)(2,1)S(1)}, u32[]{:S(2)}, u32[]{:S(2)}) collective-permute-start(bf16[576,128]{1,0:T(8,128)(2,1)S(1)} %bitcast.8), channel_id=1, source_target_pairs={{0,1},{1,0},{2,3},{3,2},{4,5},{5,4},{6,7},{7,6},{8,9},{9,8},{10,11... | collective-permute-start | bytes 442376 | tf_op jit(solution)/shard_map/ppermute | solution.py:242
  86.0 25.1 %copy-start.1 = (s32[64]{0:T(128)S(1)}, s32[64]{0:T(128)}, u32[]{:S(2)}) copy-start(s32[64]{0:T(128)} %order_ref.3) | copy-start | bytes 772

commit v5 on v4

--- a/solution.py
+++ b/solution.py
@@ -176,7 +176,10 @@
     lax.fori_loop(0, slots_ref.shape[0], body, 0, unroll=8)
 
 
-def master_kernel(order_ref, returned_ref, master_ref, out_ref, ready_ref, sem):
+def master_kernel(order_ref, returned_ref, master_ref, update_ref, out_ref, owned_ref, ready_ref, sem, owned_sem):
+    owned = pltpu.make_async_copy(update_ref, owned_ref, owned_sem)
+    owned.start()
+
     def body(slot, carry):
         matrix = order_ref[slot]
         ready_ref[matrix] = master_ref[matrix] * (1.0 - learn_rate * weight_decay) - learn_rate * returned_ref[
@@ -187,6 +190,7 @@
 
     lax.fori_loop(0, returned_ref.shape[0], body, 0, unroll=4)
     pltpu.make_async_copy(ready_ref, out_ref, sem).wait()
+    owned.wait()
 
 
 def limit(mib):
@@ -211,8 +215,10 @@
         out_shape=jax.ShapeDtypeStruct(momentum.shape, momentum.dtype),
         in_specs=[smem(), vmem()],
         out_specs=vmem(),
+        compiler_params=limit(53),
         name="gather",
     )(owner_order, momentum)
+    core, slotted = lax.optimization_barrier((core, slotted))
     owned = lax.all_to_all(slotted, "dp", split_axis=0, concat_axis=0, tiled=True)
     owned = owned.reshape(slots * rows, columns)
     packed = jax.ShapeDtypeStruct((HALF_ROWS, EDGE), jnp.bfloat16)
@@ -241,7 +247,7 @@
     mine = mine.reshape(HALF_ROWS, EDGE)
     other = lax.ppermute(mine, "core", swap)
     edge = owned.shape[0]
-    owned_update = pl.pallas_call(
+    update = pl.pallas_call(
         update_kernel,
         out_shape=jax.ShapeDtypeStruct(owned.shape, jnp.bfloat16),
         in_specs=[smem(), vmem(), vmem(), vmem()],
@@ -254,17 +260,24 @@
         name="update",
     )(core, mine, other, owned)
     returned = lax.all_to_all(
-        owned_update.reshape(slots, rows, columns), "dp", split_axis=0, concat_axis=0, tiled=True
+        update.reshape(slots, rows, columns), "dp", split_axis=0, concat_axis=0, tiled=True
     )
-    new_master = pl.pallas_call(
+    new_master, owned_update = pl.pallas_call(
         master_kernel,
-        out_shape=jax.ShapeDtypeStruct(master.shape, jnp.float32),
-        in_specs=[smem(), vmem(), vmem()],
-        out_specs=pl.BlockSpec(memory_space=pl.ANY),
-        scratch_shapes=[pltpu.VMEM(master.shape, jnp.float32), pltpu.SemaphoreType.DMA],
+        out_shape=(
+            jax.ShapeDtypeStruct(master.shape, jnp.float32),
+            jax.ShapeDtypeStruct(update.shape, update.dtype),
+        ),
+        in_specs=[smem(), vmem(), vmem(), vmem()],
+        out_specs=(pl.BlockSpec(memory_space=pl.ANY),) * 2,
+        scratch_shapes=[
+            pltpu.VMEM(master.shape, jnp.float32),
+            pltpu.SemaphoreType.DMA,
+            pltpu.SemaphoreType.DMA,
+        ],
         compiler_params=limit(8),
         name="master",
-    )(owner_order, returned, master)
+    )(owner_order, returned, master, update)
     return (new_master, owned_update[None])
 
 

time: 113 us -> 112 us (level)
  blocking collectives: 53 us -> 94.9 us
  starting transfers between devices: 27 us -> 3.96 us
  waiting for transfers between devices: 22.1 us -> 2.67 us
  Pallas kernels: 9.72 us -> 8.33 us
    all_to_all x1 -> x2, blocking collectives: 25.1 us -> 67 us  [the longest x1 42.3 us: shards(): lax.all_to_all(slotted, 'dp', split_axis=0, concat_axis=0, tiled=True)]
    all_to_all x1 -> x0, starting transfers between devices: 23.1 us -> none  [shards(): lax.all_to_all(slotted, 'dp', split_axis=0, concat_axis=0, tiled=True)]
    all_to_all x1 -> x0, waiting for transfers between devices: 19.4 us -> none  [shards(): lax.all_to_all(slotted, 'dp', split_axis=0, concat_axis=0, tiled=True)]
  transfers between devices with their start and end apart: 3 -> 2, of which waited for: 3 -> 2; matrix products, arithmetic and copies ran while one was open for 0% -> 0% of each run, Pallas kernels for 0% -> 0%
where the time goes in v5:
time: 112 us; the launch traced here: 111 us
  blocking collectives  94.9 us (85%)
  Pallas kernels  8.33 us (7%)
  starting transfers between devices  3.96 us (4%)
  waiting for transfers between devices  2.67 us (2%)
    all_to_all x1, blocking collectives, shards(): lax.all_to_all(slotted, 'dp', split_axis=0, concat_axis=0, tiled=True)  42.3 us
    all_to_all x1, blocking collectives, shards(): lax.all_to_all(update.reshape(slots, rows, columns), 'dp', split_axis=0,...  24.7 us
    all_to_all x1, blocking collectives, shards(): parts = lax.all_to_all(pair, 'x', split_axis=0, concat_axis=0, tiled=True)  16.3 us
    all_to_all x1, blocking collectives, shards(): mine = lax.all_to_all(spread, 'x', split_axis=0, concat_axis=0, tiled=True)  11.6 us
    pallas_call x1, Pallas kernels, shards(): pl.pallas_call(update_kernel, out_shape=jax.ShapeDtypeStruct(owned.shape,...  4.92 us
  transfers between devices with their start and end apart: 2, of which 2 were waited for; matrix products, arithmetic and copies ran while one was open for 0% of the time, Pallas kernels for 0%

profile of v5, /device:TPU:32, one launch (start us, length us, event | category | flops | bytes accessed | tf_op | source)
XLA Modules:
  0.0 111.3 jit_solution(3964176599408450064)
XLA Ops:
  0.6 0.0 copy-start.1
  0.6 0.6 copy-done.1
  1.3 1.2 %gather.1 = bf16[64,8,512]{2,1,0:T(8,128)(2,1)S(1)} custom-call(s32[64]{0:T(128)S(1)} %copy-done.1, bf16[64,8,512]{2,1,0:T(8,128)(2,1)} %source_ref.1), custom_call_target="tpu_custom_call" | custom-call | tf_op jit(solution)/shard_map/gather/pallas_call | solution.py:213
  2.5 42.3 %all_to_all.20 = bf16[64,8,512]{2,1,0:T(8,128)(2,1)S(1)} all-to-all(bf16[64,8,512]{2,1,0:T(8,128)(2,1)S(1)} %gather.1), channel_id=1, replica_groups=mesh['dp'=64,'x'=8,'core'=2] {'dp'}, dimensions={0} | all-to-all | bytes 1048576 | tf_op jit(solution)/shard_map/all_to_all | solution.py:222
  44.7 0.6 gram.1
  45.3 1.9 %collective-permute-start = (bf16[576,128]{1,0:T(8,128)(2,1)S(1)}, bf16[576,128]{1,0:T(8,128)(2,1)S(1)}, u32[]{:S(2)}, u32[]{:S(2)}) collective-permute-start(bf16[576,128]{1,0:T(8,128)(2,1)S(1)} %get-tuple-element.11), channel_id=1, source_target_pairs={{0,1},{1,0},{2,3},{3,2},{4,5},{5,4},{6,7},{7,6},{8,9},{9,8},{10,11... | collective-permute-start | bytes 442376 | tf_op jit(solution)/shard_map/ppermute | solution.py:234
  47.2 1.3 %collective-permute-done = bf16[576,128]{1,0:T(8,128)(2,1)S(1)} collective-permute-done((bf16[576,128]{1,0:T(8,128)(2,1)S(1)}, bf16[576,128]{1,0:T(8,128)(2,1)S(1)}, u32[]{:S(2)}, u32[]{:S(2)}) %collective-permute-start) | collective-permute-done | bytes 147488 | tf_op jit(solution)/shard_map/ppermute | solution.py:234
  48.6 16.3 %all_to_all.21.parts_ref = bf16[8,72,128]{2,1,0:T(8,128)(2,1)S(1)} all-to-all(bf16[8,72,128]{2,1,0:T(8,128)(2,1)S(1)} %bitcast.11), channel_id=1, replica_groups=mesh['dp'=64,'x'=8,'core'=2] {'x'}, dimensions={0} | all-to-all | bytes 294912 | tf_op jit(solution)/shard_map/all_to_all | solution.py:237
  64.9 11.6 %all_to_all.22 = bf16[8,72,128]{2,1,0:T(8,128)(2,1)S(1)} all-to-all(bf16[8,72,128]{2,1,0:T(8,128)(2,1)S(1)} %sum.1), channel_id=1, replica_groups=mesh['dp'=64,'x'=8,'core'=2] {'x'}, dimensions={0} | all-to-all | bytes 294912 | tf_op jit(solution)/shard_map/all_to_all | solution.py:246
  76.6 0.0 copy-start
  76.6 2.0 %collective-permute-start.1 = (bf16[576,128]{1,0:T(8,128)(2,1)S(1)}, bf16[576,128]{1,0:T(8,128)(2,1)S(1)}, u32[]{:S(2)}, u32[]{:S(2)}) collective-permute-start(bf16[576,128]{1,0:T(8,128)(2,1)S(1)} %bitcast.9), channel_id=1, source_target_pairs={{0,1},{1,0},{2,3},{3,2},{4,5},{5,4},{6,7},{7,6},{8,9},{9,8},{10,11... | collective-permute-start | bytes 442376 | tf_op jit(solution)/shard_map/ppermute | solution.py:248
  78.6 1.3 %collective-permute-done.1.other_ref = bf16[576,128]{1,0:T(8,128)(2,1)S(1)} collective-permute-done((bf16[576,128]{1,0:T(8,128)(2,1)S(1)}, bf16[576,128]{1,0:T(8,128)(2,1)S(1)}, u32[]{:S(2)}, u32[]{:S(2)}) %collective-permute-start.1) | collective-permute-done | bytes 147488 | tf_op jit(solution)/shard_map/ppermute | solution.py:248
  80.0 4.9 %update.1.update_ref = bf16[512,512]{1,0:T(8,128)(2,1)S(1)} custom-call(s32[1]{0:T(128)} %bitcast.core_ref, bf16[576,128]{1,0:T(8,128)(2,1)S(1)} %bitcast.10, bf16[576,128]{1,0:T(8,128)(2,1)S(1)} %collective-permute-done.1.other_ref, bf16[512,512]{1,0:T(8,128)(2,1)S(1)} %bitcast.8), custom_call_target="tpu_custom_call" | custom-call | tf_op jit(solution)/shard_map/update/pallas_call | solution.py:250
  84.9 24.7 %all_to_all.23.returned_ref = bf16[64,8,512]{2,1,0:T(8,128)(2,1)S(1)} all-to-all(bf16[64,8,512]{2,1,0:T(8,128)(2,1)S(1)} %bitcast.6), channel_id=1, replica_groups=mesh['dp'=64,'x'=8,'core'=2] {'dp'}, dimensions={0} | all-to-all | bytes 1048576 | tf_op jit(solution)/shard_map/all_to_all | solution.py:262
  109.6 0.0 copy-done
  109.6 1.7 %master.1 = (f32[64,8,512]{2,1,0:T(8,128)}, bf16[512,512]{1,0:T(8,128)(2,1)}) custom-call(s32[64]{0:T(128)S(1)} %copy-done.1, bf16[64,8,512]{2,1,0:T(8,128)(2,1)S(1)} %all_to_all.23.returned_ref, f32[64,8,512]{2,1,0:T(8,128)S(1)} %copy-done, bf16[512,512]{1,0:T(8,128)(2,1)S(1)} %update.1.update_ref), custom_call_target="tpu_custom_call" | custom-call | tf_op jit(solution)/shard_map/master/pallas_call | solution.py:265
  (2 shorter events, 0.1 us)
Async XLA Ops:
  0.6 0.7 copy-start.1
  45.3 3.3 %collective-permute-start = (bf16[576,128]{1,0:T(8,128)(2,1)S(1)}, bf16[576,128]{1,0:T(8,128)(2,1)S(1)}, u32[]{:S(2)}, u32[]{:S(2)}) collective-permute-start(bf16[576,128]{1,0:T(8,128)(2,1)S(1)} %get-tuple-element.11), channel_id=1, source_target_pairs={{0,1},{1,0},{2,3},{3,2},{4,5},{5,4},{6,7},{7,6},{8,9},{9,8},{10,11... | collective-permute-start | bytes 442376 | tf_op jit(solution)/shard_map/ppermute | solution.py:234
  76.6 33.0 %copy-start = (f32[64,8,512]{2,1,0:T(8,128)S(1)}, f32[64,8,512]{2,1,0:T(8,128)}, u32[]{:S(2)}) copy-start(f32[64,8,512]{2,1,0:T(8,128)} %master_ref.1) | copy-start | bytes 3145732
  76.6 3.4 %collective-permute-start.1 = (bf16[576,128]{1,0:T(8,128)(2,1)S(1)}, bf16[576,128]{1,0:T(8,128)(2,1)S(1)}, u32[]{:S(2)}, u32[]{:S(2)}) collective-permute-start(bf16[576,128]{1,0:T(8,128)(2,1)S(1)} %bitcast.9), channel_id=1, source_target_pairs={{0,1},{1,0},{2,3},{3,2},{4,5},{5,4},{6,7},{7,6},{8,9},{9,8},{10,11... | collective-permute-start | bytes 442376 | tf_op jit(solution)/shard_map/ppermute | solution.py:248

commit v6 on v5

--- a/solution.py
+++ b/solution.py
@@ -217,7 +217,7 @@
         out_specs=vmem(),
         compiler_params=limit(53),
         name="gather",
-    )(owner_order, momentum)
+    )(pltpu.with_memory_space_constraint(owner_order, pltpu.HBM), momentum)
     core, slotted = lax.optimization_barrier((core, slotted))
     owned = lax.all_to_all(slotted, "dp", split_axis=0, concat_axis=0, tiled=True)
     owned = owned.reshape(slots * rows, columns)

time: 112 us -> 111 us (level)
  no operation moved by 1% of the time
where the time goes in v6:
time: 111 us
  blocking collectives  94.9 us (85%)
  Pallas kernels  8.33 us (8%)
  starting transfers between devices  3.96 us (4%)
  waiting for transfers between devices  2.67 us (2%)
    all_to_all x1, blocking collectives, shards(): lax.all_to_all(slotted, 'dp', split_axis=0, concat_axis=0, tiled=True)  42.3 us
    all_to_all x1, blocking collectives, shards(): lax.all_to_all(update.reshape(slots, rows, columns), 'dp', split_axis=0,...  24.7 us
    all_to_all x1, blocking collectives, shards(): parts = lax.all_to_all(pair, 'x', split_axis=0, concat_axis=0, tiled=True)  16.3 us
    all_to_all x1, blocking collectives, shards(): mine = lax.all_to_all(spread, 'x', split_axis=0, concat_axis=0, tiled=True)  11.6 us
    pallas_call x1, Pallas kernels, shards(): pl.pallas_call(update_kernel, out_shape=jax.ShapeDtypeStruct(owned.shape,...  4.92 us
  transfers between devices with their start and end apart: 2, of which 2 were waited for; matrix products, arithmetic and copies ran while one was open for 0% of the time, Pallas kernels for 0%

profile of v6, /device:TPU:32, one launch (start us, length us, event | category | flops | bytes accessed | tf_op | source)
XLA Modules:
  0.0 110.6 jit_solution(17498130169883336849)
XLA Ops:
  0.6 1.2 %gather.1 = bf16[64,8,512]{2,1,0:T(8,128)(2,1)S(1)} custom-call(s32[64]{0:T(128)} %order_ref.3, bf16[64,8,512]{2,1,0:T(8,128)(2,1)} %source_ref.1), custom_call_target="tpu_custom_call" | custom-call | tf_op jit(solution)/shard_map/gather/pallas_call | solution.py:213
  1.8 42.3 %all_to_all.20 = bf16[64,8,512]{2,1,0:T(8,128)(2,1)S(1)} all-to-all(bf16[64,8,512]{2,1,0:T(8,128)(2,1)S(1)} %gather.1), channel_id=1, replica_groups=mesh['dp'=64,'x'=8,'core'=2] {'dp'}, dimensions={0} | all-to-all | bytes 1048576 | tf_op jit(solution)/shard_map/all_to_all | solution.py:222
  44.1 0.6 gram.1
  44.6 1.9 %collective-permute-start = (bf16[576,128]{1,0:T(8,128)(2,1)S(1)}, bf16[576,128]{1,0:T(8,128)(2,1)S(1)}, u32[]{:S(2)}, u32[]{:S(2)}) collective-permute-start(bf16[576,128]{1,0:T(8,128)(2,1)S(1)} %get-tuple-element.11), channel_id=1, source_target_pairs={{0,1},{1,0},{2,3},{3,2},{4,5},{5,4},{6,7},{7,6},{8,9},{9,8},{10,11... | collective-permute-start | bytes 442376 | tf_op jit(solution)/shard_map/ppermute | solution.py:234
  46.6 1.3 %collective-permute-done = bf16[576,128]{1,0:T(8,128)(2,1)S(1)} collective-permute-done((bf16[576,128]{1,0:T(8,128)(2,1)S(1)}, bf16[576,128]{1,0:T(8,128)(2,1)S(1)}, u32[]{:S(2)}, u32[]{:S(2)}) %collective-permute-start) | collective-permute-done | bytes 147488 | tf_op jit(solution)/shard_map/ppermute | solution.py:234
  48.0 16.3 %all_to_all.21.parts_ref = bf16[8,72,128]{2,1,0:T(8,128)(2,1)S(1)} all-to-all(bf16[8,72,128]{2,1,0:T(8,128)(2,1)S(1)} %bitcast.11), channel_id=1, replica_groups=mesh['dp'=64,'x'=8,'core'=2] {'x'}, dimensions={0} | all-to-all | bytes 294912 | tf_op jit(solution)/shard_map/all_to_all | solution.py:237
  64.3 11.6 %all_to_all.22 = bf16[8,72,128]{2,1,0:T(8,128)(2,1)S(1)} all-to-all(bf16[8,72,128]{2,1,0:T(8,128)(2,1)S(1)} %sum.1), channel_id=1, replica_groups=mesh['dp'=64,'x'=8,'core'=2] {'x'}, dimensions={0} | all-to-all | bytes 294912 | tf_op jit(solution)/shard_map/all_to_all | solution.py:246
  75.9 0.0 copy-start
  75.9 2.0 %collective-permute-start.1 = (bf16[576,128]{1,0:T(8,128)(2,1)S(1)}, bf16[576,128]{1,0:T(8,128)(2,1)S(1)}, u32[]{:S(2)}, u32[]{:S(2)}) collective-permute-start(bf16[576,128]{1,0:T(8,128)(2,1)S(1)} %bitcast.9), channel_id=1, source_target_pairs={{0,1},{1,0},{2,3},{3,2},{4,5},{5,4},{6,7},{7,6},{8,9},{9,8},{10,11... | collective-permute-start | bytes 442376 | tf_op jit(solution)/shard_map/ppermute | solution.py:248
  78.0 1.3 %collective-permute-done.1.other_ref = bf16[576,128]{1,0:T(8,128)(2,1)S(1)} collective-permute-done((bf16[576,128]{1,0:T(8,128)(2,1)S(1)}, bf16[576,128]{1,0:T(8,128)(2,1)S(1)}, u32[]{:S(2)}, u32[]{:S(2)}) %collective-permute-start.1) | collective-permute-done | bytes 147488 | tf_op jit(solution)/shard_map/ppermute | solution.py:248
  79.3 4.9 %update.1.update_ref = bf16[512,512]{1,0:T(8,128)(2,1)S(1)} custom-call(s32[1]{0:T(128)} %bitcast.core_ref, bf16[576,128]{1,0:T(8,128)(2,1)S(1)} %bitcast.10, bf16[576,128]{1,0:T(8,128)(2,1)S(1)} %collective-permute-done.1.other_ref, bf16[512,512]{1,0:T(8,128)(2,1)S(1)} %bitcast.8), custom_call_target="tpu_custom_call" | custom-call | tf_op jit(solution)/shard_map/update/pallas_call | solution.py:250
  84.2 0.0 copy-start.1
  84.2 24.7 %all_to_all.23.returned_ref = bf16[64,8,512]{2,1,0:T(8,128)(2,1)S(1)} all-to-all(bf16[64,8,512]{2,1,0:T(8,128)(2,1)S(1)} %bitcast.6), channel_id=1, replica_groups=mesh['dp'=64,'x'=8,'core'=2] {'dp'}, dimensions={0} | all-to-all | bytes 1048576 | tf_op jit(solution)/shard_map/all_to_all | solution.py:262
  109.0 0.0 copy-done
  109.0 0.0 copy-done.1
  109.0 1.7 %master.1 = (f32[64,8,512]{2,1,0:T(8,128)}, bf16[512,512]{1,0:T(8,128)(2,1)}) custom-call(s32[64]{0:T(128)S(1)} %copy-done.1, bf16[64,8,512]{2,1,0:T(8,128)(2,1)S(1)} %all_to_all.23.returned_ref, f32[64,8,512]{2,1,0:T(8,128)S(1)} %copy-done, bf16[512,512]{1,0:T(8,128)(2,1)S(1)} %update.1.update_ref), custom_call_target="tpu_custom_call" | custom-call | tf_op jit(solution)/shard_map/master/pallas_call | solution.py:265
  (2 shorter events, 0.1 us)
Async XLA Ops:
  44.6 3.3 %collective-permute-start = (bf16[576,128]{1,0:T(8,128)(2,1)S(1)}, bf16[576,128]{1,0:T(8,128)(2,1)S(1)}, u32[]{:S(2)}, u32[]{:S(2)}) collective-permute-start(bf16[576,128]{1,0:T(8,128)(2,1)S(1)} %get-tuple-element.11), channel_id=1, source_target_pairs={{0,1},{1,0},{2,3},{3,2},{4,5},{5,4},{6,7},{7,6},{8,9},{9,8},{10,11... | collective-permute-start | bytes 442376 | tf_op jit(solution)/shard_map/ppermute | solution.py:234
  75.9 33.1 %copy-start = (f32[64,8,512]{2,1,0:T(8,128)S(1)}, f32[64,8,512]{2,1,0:T(8,128)}, u32[]{:S(2)}) copy-start(f32[64,8,512]{2,1,0:T(8,128)} %master_ref.1) | copy-start | bytes 3145732
  75.9 3.4 %collective-permute-start.1 = (bf16[576,128]{1,0:T(8,128)(2,1)S(1)}, bf16[576,128]{1,0:T(8,128)(2,1)S(1)}, u32[]{:S(2)}, u32[]{:S(2)}) collective-permute-start(bf16[576,128]{1,0:T(8,128)(2,1)S(1)} %bitcast.9), channel_id=1, source_target_pairs={{0,1},{1,0},{2,3},{3,2},{4,5},{5,4},{6,7},{7,6},{8,9},{9,8},{10,11... | collective-permute-start | bytes 442376 | tf_op jit(solution)/shard_map/ppermute | solution.py:248
  84.2 24.8 %copy-start.1 = (s32[64]{0:T(128)S(1)}, s32[64]{0:T(128)}, u32[]{:S(2)}) copy-start(s32[64]{0:T(128)} %order_ref.3) | copy-start | bytes 772
